TPU v7x, 32 devices: a whole 2x2x4 slice. The times are simulated.
32 devices in a mesh: dp: 16 (over z, x, core), tensor: 2 (over y).
Axes of the slice: x: 2, y: 2, z: 4, core: 2. Of those that a mesh axis runs over, the one named last changes fastest.
Arguments:
- tokens: bfloat16 [16384, 768], P(('dp', 'tensor')), may hold values from -6 to 6
- lengths: int32 [32], P('dp'), may hold values from 224 to 512, as said below
- cotangent: bfloat16 [16384, 768], P(('dp', 'tensor')), may hold values from -6 to 6
- norm_gain: float32 [2, 2, 768], replicated, may hold values from 0.25 to 1.75
- norm_shift: float32 [2, 2, 768], replicated, may hold values from -1.75 to 1.75
- qkv_weight: bfloat16 [2, 768, 3, 768], P(None, 'dp', None, 'tensor'), may hold values from -0.21875 to 0.21875
- qv_bias: float32 [2, 2, 768], P(None, None, 'tensor'), may hold values from -1.75 to 1.75
- out_weight: bfloat16 [2, 768, 768], P(None, 'tensor', 'dp'), may hold values from -2 to 2
- up_weight: bfloat16 [2, 768, 3072], P(None, 'dp', 'tensor'), may hold values from -0.21875 to 0.21875
- up_bias: float32 [2, 3072], P(None, 'tensor'), may hold values from -1.75 to 1.75
- down_weight: bfloat16 [2, 3072, 768], P(None, 'tensor', 'dp'), may hold values from -0.109375 to 0.109375
- out_bias: float32 [2, 2, 768], replicated, may hold values from -1.75 to 1.75
Outputs:
- final: bfloat16 [16384, 768], P(('dp', 'tensor'))
- token_grad: float32 [16384, 768], P(('dp', 'tensor'))
- grad_norm_gain: float32 [2, 2, 768], replicated
- grad_norm_shift: float32 [2, 2, 768], replicated
- grad_qkv_weight: float32 [2, 768, 3, 768], P(None, 'dp', None, 'tensor')
- grad_qv_bias: float32 [2, 2, 768], P(None, None, 'tensor')
- grad_out_weight: float32 [2, 768, 768], P(None, 'tensor', 'dp')
- grad_up_weight: float32 [2, 768, 3072], P(None, 'dp', 'tensor')
- grad_up_bias: float32 [2, 3072], P(None, 'tensor')
- grad_down_weight: float32 [2, 3072, 768], P(None, 'tensor', 'dp')
- grad_out_bias: float32 [2, 2, 768], replicated
Inputs may be any that keep to these rules, and one draw needn't show every extreme that they name: `lengths`: each clip holds 224 to 512 patches; clip 0 holds exactly 512.
All inputs are finite; a program needn't handle non-finite values.
Results may differ from a plain program's by a relative error of at most 0.015.
Values may be sent and summed in bfloat16 or wider, within the bound.
A program may use at most 192 MiB of HBM per device.

v0:
```python
import jax
import jax.numpy as jnp
from jax import lax
from jax.sharding import PartitionSpec as P

HEAD_DIM = 64
SLOT = 512


EPSILON = 1e-06


def layer_norm(inputs, gain_row, shift_row):
    centered = inputs - jnp.mean(inputs, axis=-1, keepdims=True)
    variance = jnp.mean(centered * centered, axis=-1, keepdims=True)
    return centered * lax.rsqrt(variance + EPSILON) * gain_row + shift_row


def gelu_exact(values):
    return jax.nn.gelu(values, approximate=False)


def contract_rows(left, right):
    return lax.dot_general(
        left, right, (((0,), (0,)), ((), ())), preferred_element_type=jnp.float32
    )


def contract_cols(left, right):
    return lax.dot_general(
        left, right, (((1,), (1,)), ((), ())), preferred_element_type=jnp.float32
    )


def attend(project, key_mask):
    row_count, _, local_width = project.shape
    local_heads = local_width // HEAD_DIM
    clip_count = key_mask.shape[0]
    blocks = project.reshape(clip_count, SLOT, 3, local_heads, HEAD_DIM)

    def one_clip(clip_item):
        clip_block, keeper = clip_item
        scores = jnp.einsum(
            "qhd,khd->hqk", clip_block[:, 0], clip_block[:, 1], preferred_element_type=jnp.float32
        ) * HEAD_DIM ** (-0.5)
        scores = jnp.where(keeper[None, None, :], scores, -1e30)
        highest = jnp.max(scores, axis=-1)
        exponent = jnp.exp(scores - highest[..., None])
        summed = jnp.sum(exponent, axis=-1)
        probability = (exponent / summed[..., None]).astype(jnp.bfloat16)
        mixture = jnp.einsum(
            "hqk,khd->qhd", probability, clip_block[:, 2], preferred_element_type=jnp.float32
        )
        return (mixture.astype(jnp.bfloat16), highest + jnp.log(summed))

    mixture, log_total = lax.map(one_clip, (blocks, key_mask))
    return (mixture.reshape(row_count, local_width), log_total)


def attend_back(project, upstream, log_total, key_mask):
    row_count, _, local_width = project.shape
    local_heads = local_width // HEAD_DIM
    clip_count = key_mask.shape[0]
    blocks = project.reshape(clip_count, SLOT, 3, local_heads, HEAD_DIM)
    upstream_blocks = upstream.reshape(clip_count, SLOT, local_heads, HEAD_DIM)
    scale = HEAD_DIM ** (-0.5)

    def one_clip(clip_item):
        clip_block, upstream_block, clip_total, keeper = clip_item
        queries = clip_block[:, 0]
        keys_block = clip_block[:, 1]
        values = clip_block[:, 2]
        scores = (
            jnp.einsum("qhd,khd->hqk", queries, keys_block, preferred_element_type=jnp.float32)
            * scale
        )
        scores = jnp.where(keeper[None, None, :], scores, -1e30)
        probability = jnp.exp(scores - clip_total[..., None])
        rounded = probability.astype(jnp.bfloat16)
        grad_values = jnp.einsum(
            "hqk,qhd->khd", rounded, upstream_block, preferred_element_type=jnp.float32
        )
        grad_probs = jnp.einsum(
            "qhd,khd->hqk", upstream_block, values, preferred_element_type=jnp.float32
        )
        centred = grad_probs - jnp.sum(probability * grad_probs, axis=-1, keepdims=True)
        grad_scores = (probability * centred).astype(jnp.bfloat16)
        grad_queries = (
            jnp.einsum("hqk,khd->qhd", grad_scores, keys_block, preferred_element_type=jnp.float32)
            * scale
        )
        grad_keys = (
            jnp.einsum("hqk,qhd->khd", grad_scores, queries, preferred_element_type=jnp.float32)
            * scale
        )
        return jnp.stack([grad_queries, grad_keys, grad_values], axis=1).astype(jnp.bfloat16)

    grads = lax.map(one_clip, (blocks, upstream_blocks, log_total, key_mask))
    return grads.reshape(row_count, 3, local_width)


def body(
    tokens,
    lengths,
    cotangent,
    norm_gain,
    norm_shift,
    qkv_weight,
    qv_bias,
    out_weight,
    up_weight,
    up_bias,
    down_weight,
    out_bias,
):
    part_index = lax.axis_index("tensor")
    own_rows = tokens.shape[0]
    layer_count = norm_gain.shape[0]
    positions = jnp.arange(SLOT, dtype=jnp.int32)
    key_mask = positions[None, :] < lengths[:, None]
    mask_all = key_mask.reshape(-1).astype(jnp.float32)
    own_mask = lax.dynamic_slice_in_dim(mask_all, part_index * own_rows, own_rows)
    stream = tokens.astype(jnp.float32)
    saved = []
    for layer_index in range(layer_count):
        weights = (
            lax.all_gather(qkv_weight[layer_index], "dp", axis=0, tiled=True),
            lax.all_gather(out_weight[layer_index], "dp", axis=1, tiled=True),
            lax.all_gather(up_weight[layer_index], "dp", axis=0, tiled=True),
            lax.all_gather(down_weight[layer_index], "dp", axis=1, tiled=True),
        )
        w_qkv, w_out, w_up, w_down = weights
        normed_own = layer_norm(
            stream, norm_gain[layer_index, 0], norm_shift[layer_index, 0]
        ).astype(jnp.bfloat16)
        normed = lax.all_gather(normed_own, "tensor", axis=0, tiled=True)
        zeros_row = jnp.zeros_like(qv_bias[layer_index, 0])
        bias_rows = jnp.stack([qv_bias[layer_index, 0], zeros_row, qv_bias[layer_index, 1]])
        project = (
            jnp.einsum("nd,dtc->ntc", normed, w_qkv, preferred_element_type=jnp.float32) + bias_rows
        ).astype(jnp.bfloat16)
        attended, log_total = attend(project, key_mask)
        branch = lax.psum_scatter(
            jnp.dot(attended, w_out, preferred_element_type=jnp.float32).astype(jnp.bfloat16),
            "tensor",
            scatter_dimension=0,
            tiled=True,
        ).astype(jnp.float32)
        middle = stream + branch + out_bias[layer_index, 0]
        normed_mid_own = layer_norm(
            middle, norm_gain[layer_index, 1], norm_shift[layer_index, 1]
        ).astype(jnp.bfloat16)
        normed_mid = lax.all_gather(normed_mid_own, "tensor", axis=0, tiled=True)
        hidden = (
            jnp.dot(normed_mid, w_up, preferred_element_type=jnp.float32) + up_bias[layer_index]
        )
        activated = gelu_exact(hidden).astype(jnp.bfloat16)
        branch_mlp = lax.psum_scatter(
            jnp.dot(activated, w_down, preferred_element_type=jnp.float32).astype(jnp.bfloat16),
            "tensor",
            scatter_dimension=0,
            tiled=True,
        ).astype(jnp.float32)
        kept_weights = None
        saved.append(
            (
                stream,
                middle,
                normed,
                project,
                attended,
                log_total,
                normed_mid,
                hidden,
                activated,
                kept_weights,
            )
        )
        stream = middle + branch_mlp + out_bias[layer_index, 1]
    final = stream.astype(jnp.bfloat16)
    gradient = cotangent.astype(jnp.float32) * own_mask[:, None]
    grad_gain = [None] * layer_count
    grad_shift = [None] * layer_count
    grad_outb = [None] * layer_count
    grad_qkv = [None] * layer_count
    grad_qvb = [None] * layer_count
    grad_wout = [None] * layer_count
    grad_wup = [None] * layer_count
    grad_upb = [None] * layer_count
    grad_wdown = [None] * layer_count
    for layer_index in reversed(range(layer_count)):
        (
            stream_in,
            middle,
            normed,
            project,
            attended,
            log_total,
            normed_mid,
            hidden,
            activated,
            kept_weights,
        ) = saved[layer_index]
        w_qkv, w_out, w_up, w_down = (
            lax.all_gather(qkv_weight[layer_index], "dp", axis=0, tiled=True),
            lax.all_gather(out_weight[layer_index], "dp", axis=1, tiled=True),
            lax.all_gather(up_weight[layer_index], "dp", axis=0, tiled=True),
            lax.all_gather(down_weight[layer_index], "dp", axis=1, tiled=True),
        )
        bias_late = jnp.sum(gradient, axis=0)
        grad_branch_mlp = lax.all_gather(
            gradient.astype(jnp.bfloat16), "tensor", axis=0, tiled=True
        )
        grad_wdown[layer_index] = contract_rows(activated, grad_branch_mlp)
        grad_act = contract_cols(grad_branch_mlp, w_down)
        gelu_pull = jax.vjp(gelu_exact, hidden)[1]
        grad_hidden = gelu_pull(grad_act)[0].astype(jnp.bfloat16)
        grad_upb[layer_index] = jnp.sum(grad_hidden.astype(jnp.float32), axis=0)
        grad_wup[layer_index] = contract_rows(normed_mid, grad_hidden)
        grad_normed_mid = lax.psum_scatter(
            contract_cols(grad_hidden, w_up).astype(jnp.bfloat16),
            "tensor",
            scatter_dimension=0,
            tiled=True,
        ).astype(jnp.float32)
        norm_pull = jax.vjp(
            layer_norm, middle, norm_gain[layer_index, 1], norm_shift[layer_index, 1]
        )[1]
        grad_mid_in, gain_late, shift_late = norm_pull(grad_normed_mid)
        grad_middle = gradient + grad_mid_in
        bias_early = jnp.sum(grad_middle, axis=0)
        grad_branch = lax.all_gather(grad_middle.astype(jnp.bfloat16), "tensor", axis=0, tiled=True)
        grad_wout[layer_index] = contract_rows(attended, grad_branch)
        grad_attended = contract_cols(grad_branch, w_out).astype(jnp.bfloat16)
        grad_project = attend_back(project, grad_attended, log_total, key_mask)
        project_sums = jnp.sum(grad_project.astype(jnp.float32), axis=0)
        grad_qvb[layer_index] = jnp.stack([project_sums[0], project_sums[2]])
        grad_qkv[layer_index] = jnp.einsum(
            "nd,ntc->dtc", normed, grad_project, preferred_element_type=jnp.float32
        )
        grad_normed = lax.psum_scatter(
            jnp.einsum(
                "ntc,dtc->nd", grad_project, w_qkv, preferred_element_type=jnp.float32
            ).astype(jnp.bfloat16),
            "tensor",
            scatter_dimension=0,
            tiled=True,
        ).astype(jnp.float32)
        first_pull = jax.vjp(
            layer_norm, stream_in, norm_gain[layer_index, 0], norm_shift[layer_index, 0]
        )[1]
        grad_first_in, gain_early, shift_early = first_pull(grad_normed)
        gradient = grad_middle + grad_first_in
        grad_gain[layer_index] = jnp.stack([gain_early, gain_late])
        grad_shift[layer_index] = jnp.stack([shift_early, shift_late])
        grad_outb[layer_index] = jnp.stack([bias_early, bias_late])
    summed_qkv, summed_wout, summed_wup, summed_wdown = (
        lax.psum_scatter(jnp.stack(grad_qkv), "dp", scatter_dimension=1, tiled=True),
        lax.psum_scatter(jnp.stack(grad_wout), "dp", scatter_dimension=2, tiled=True),
        lax.psum_scatter(jnp.stack(grad_wup), "dp", scatter_dimension=1, tiled=True),
        lax.psum_scatter(jnp.stack(grad_wdown), "dp", scatter_dimension=2, tiled=True),
    )
    summed_gain, summed_shift, summed_outb = lax.psum(
        (jnp.stack(grad_gain), jnp.stack(grad_shift), jnp.stack(grad_outb)), ("dp", "tensor")
    )
    summed_qvb, summed_upb = lax.psum((jnp.stack(grad_qvb), jnp.stack(grad_upb)), "dp")
    return (
        final,
        gradient,
        summed_gain,
        summed_shift,
        summed_qkv,
        summed_qvb,
        summed_wout,
        summed_wup,
        summed_upb,
        summed_wdown,
        summed_outb,
    )


def solution(mesh):
    return jax.shard_map(
        body,
        mesh=mesh,
        in_specs=(
            P(("dp", "tensor"), None),
            P("dp"),
            P(("dp", "tensor"), None),
            P(),
            P(),
            P(None, "dp", None, "tensor"),
            P(None, None, "tensor"),
            P(None, "tensor", "dp"),
            P(None, "dp", "tensor"),
            P(None, "tensor"),
            P(None, "tensor", "dp"),
            P(),
        ),
        out_specs=(
            P(("dp", "tensor"), None),
            P(("dp", "tensor"), None),
            P(),
            P(),
            P(None, "dp", None, "tensor"),
            P(None, None, "tensor"),
            P(None, "tensor", "dp"),
            P(None, "dp", "tensor"),
            P(None, "tensor"),
            P(None, "tensor", "dp"),
            P(),
        ),
        check_vma=False,
    )
```

profile of v0, /device:TPU:0, one launch (start us, length us, event | category | flops | bytes accessed | tf_op | source)
XLA Modules:
  0.0 1359.7 jit_solution(5959392380114156507)
XLA Ops:
  17.7 26.1 %all-gather.1 = bf16[1,384,768]{1,2,0:T(8,128)(2,1)} all-gather(bf16[1,384,48]{1,2,0:T(8,128)(2,1)S(1)} %get-tuple-element.348), channel_id=3, replica_groups=mesh['dp'=16,'tensor'=2] {'dp'}, dimensions={2}, use_global_device_ids=true | all-gather | bytes 626688 | tf_op jit(solution)/shard_map/all_gather | solution.py:128
  46.0 43.3 %all-gather.39.cloned.1.call-done = bf16[1,768,3,384]{3,1,2,0:T(8,128)(2,1)} async-done(((bf16[1,48,3,384]{3,1,2,0:T(8,128)(2,1)}), bf16[1,768,3,384]{3,1,2,0:T(8,128)(2,1)}) %all-gather.39.cloned.1.call-update) | async-done | bytes 1769488 | tf_op jit(solution)/shard_map/all_gather | solution.py:127
  118.1 23.4 %reduce-scatter.11.cloned.1.call-done = bf16[512,768]{1,0:T(8,128)(2,1)} async-done(((bf16[1024,768]{1,0:T(8,128)(2,1)}), bf16[512,768]{1,0:T(8,128)(2,1)}) %reduce-scatter.11.cloned.1.call-update) | async-done | bytes 786448 | tf_op jit(solution)/shard_map/reduce_scatter | solution.py:143
  147.1 39.8 %all-gather.41.cloned.1.call-done = bf16[1,768,1536]{2,1,0:T(8,128)(2,1)} async-done(((bf16[1,48,1536]{2,1,0:T(8,128)(2,1)}), bf16[1,768,1536]{2,1,0:T(8,128)(2,1)}) %all-gather.41.cloned.1.call-update) | async-done | bytes 2359312 | tf_op jit(solution)/shard_map/all_gather | solution.py:129
  186.9 28.1 %all-gather.25.cloned.1.call-done = bf16[1024,768]{1,0:T(8,128)(2,1)} async-done(((bf16[512,768]{1,0:T(8,128)(2,1)}), bf16[1024,768]{1,0:T(8,128)(2,1)}) %all-gather.25.cloned.1.call-update) | async-done | bytes 1572880 | tf_op jit(solution)/shard_map/all_gather | solution.py:153
  234.9 25.4 %all-gather.43.cloned.1.call-done = bf16[1,1536,768]{1,2,0:T(8,128)(2,1)} async-done(((bf16[1,1536,48]{1,2,0:T(8,128)(2,1)}), bf16[1,1536,768]{1,2,0:T(8,128)(2,1)}) %all-gather.43.cloned.1.call-update) | async-done | bytes 2359312 | tf_op jit(solution)/shard_map/all_gather | solution.py:130
  267.5 24.2 %reduce-scatter.13.cloned.1.call-done = bf16[512,768]{1,0:T(8,128)(2,1)} async-done(((bf16[1024,768]{1,0:T(8,128)(2,1)}), bf16[512,768]{1,0:T(8,128)(2,1)}) %reduce-scatter.13.cloned.1.call-update) | async-done | bytes 786448 | tf_op jit(solution)/shard_map/reduce_scatter | solution.py:158
  295.7 25.0 %all-gather.5 = bf16[1,384,768]{1,2,0:T(8,128)(2,1)} all-gather(bf16[1,384,48]{1,2,0:T(8,128)(2,1)S(1)} %get-tuple-element.347), channel_id=7, replica_groups=mesh['dp'=16,'tensor'=2] {'dp'}, dimensions={2}, use_global_device_ids=true | all-gather | bytes 626688 | tf_op jit(solution)/shard_map/all_gather | solution.py:128
  335.2 28.3 %all-gather.27.cloned.1.call-done = bf16[1024,768]{1,0:T(8,128)(2,1)} async-done(((bf16[512,768]{1,0:T(8,128)(2,1)}), bf16[1024,768]{1,0:T(8,128)(2,1)}) %all-gather.27.cloned.1.call-update) | async-done | bytes 1572880 | tf_op jit(solution)/shard_map/all_gather | solution.py:136
  391.0 25.5 %reduce-scatter.15.cloned.1.call-done = bf16[512,768]{1,0:T(8,128)(2,1)} async-done(((bf16[1024,768]{1,0:T(8,128)(2,1)}), bf16[512,768]{1,0:T(8,128)(2,1)}) %reduce-scatter.15.cloned.1.call-update) | async-done | bytes 786448 | tf_op jit(solution)/shard_map/reduce_scatter | solution.py:143
  422.9 39.1 %all-gather.47.cloned.1.call-done = bf16[1,768,1536]{2,1,0:T(8,128)(2,1)} async-done(((bf16[1,48,1536]{2,1,0:T(8,128)(2,1)}), bf16[1,768,1536]{2,1,0:T(8,128)(2,1)}) %all-gather.47.cloned.1.call-update) | async-done | bytes 2359312 | tf_op jit(solution)/shard_map/all_gather | solution.py:129
  462.0 28.1 %all-gather.29.cloned.1.call-done = bf16[1024,768]{1,0:T(8,128)(2,1)} async-done(((bf16[512,768]{1,0:T(8,128)(2,1)}), bf16[1024,768]{1,0:T(8,128)(2,1)}) %all-gather.29.cloned.1.call-update) | async-done | bytes 1572880 | tf_op jit(solution)/shard_map/all_gather | solution.py:153
  518.9 45.3 %all-gather.49.cloned.1.call-done = bf16[1,1536,768]{1,2,0:T(8,128)(2,1)} async-done(((bf16[1,1536,48]{1,2,0:T(8,128)(2,1)}), bf16[1,1536,768]{1,2,0:T(8,128)(2,1)}) %all-gather.49.cloned.1.call-update) | async-done | bytes 2359312 | tf_op jit(solution)/shard_map/all_gather | solution.py:130
  610.0 23.9 %reduce-scatter.17.cloned.1.call-done = bf16[512,768]{1,0:T(8,128)(2,1)} async-done(((bf16[1024,768]{1,0:T(8,128)(2,1)}), bf16[512,768]{1,0:T(8,128)(2,1)}) %reduce-scatter.17.cloned.1.call-update) | async-done | bytes 786448 | tf_op jit(solution)/shard_map/reduce_scatter | solution.py:158
  640.1 27.1 %all-gather.33.cloned.1.call-done = bf16[1024,768]{1,0:T(8,128)(2,1)} async-done(((bf16[512,768]{1,0:T(8,128)(2,1)}), bf16[1024,768]{1,0:T(8,128)(2,1)}) %all-gather.33.cloned.1.call-update) | async-done | bytes 1572880 | tf_op jit(solution)/shard_map/all_gather | solution.py:232
  709.3 25.8 %reduce-scatter.21.cloned.1.call-done = bf16[512,768]{1,0:T(8,128)(2,1)} async-done(((bf16[1024,768]{1,0:T(8,128)(2,1)}), bf16[512,768]{1,0:T(8,128)(2,1)}) %reduce-scatter.21.cloned.1.call-update) | async-done | bytes 786448 | tf_op jit(solution)/shard_map/reduce_scatter | solution.py:241
  742.3 27.3 %all-gather.35.cloned.1.call-done = bf16[1024,768]{1,0:T(8,128)(2,1)} async-done(((bf16[512,768]{1,0:T(8,128)(2,1)}), bf16[1024,768]{1,0:T(8,128)(2,1)}) %all-gather.35.cloned.1.call-update) | async-done | bytes 1572880 | tf_op jit(solution)/shard_map/all_gather | solution.py:211
  783.6 26.1 %reduce-scatter.23.cloned.1.call-done = bf16[512,768]{1,0:T(8,128)(2,1)} async-done(((bf16[1024,768]{1,0:T(8,128)(2,1)}), bf16[512,768]{1,0:T(8,128)(2,1)}) %reduce-scatter.23.cloned.1.call-update) | async-done | bytes 786448 | tf_op jit(solution)/shard_map/reduce_scatter | solution.py:220
  815.8 27.3 %all-gather.37.cloned.1.call-done = bf16[1024,768]{1,0:T(8,128)(2,1)} async-done(((bf16[512,768]{1,0:T(8,128)(2,1)}), bf16[1024,768]{1,0:T(8,128)(2,1)}) %all-gather.37.cloned.1.call-update) | async-done | bytes 1572880 | tf_op jit(solution)/shard_map/all_gather | solution.py:232
  950.0 64.8 %all-reduce.3 = (f32[2,2,384]{2,1,0:T(2,128)}, f32[2,1536]{1,0:T(2,128)}) all-reduce(f32[2,2,384]{2,1,0:T(2,128)S(1)} %pad_maximum_fusion.10, f32[2,1536]{1,0:T(2,128)S(1)} %pad_maximum_fusion.6), channel_id=1, replica_groups=mesh['dp'=16,'tensor'=2] {'dp'}, use_global_device_ids=true, to_apply=%region_51.52 | all-reduce | flops 4608 | bytes 36864 | tf_op jit(solution)/shard_map/psum | solution.py:266
  1018.8 38.8 %all-reduce.2 = (f32[2,2,768]{2,1,0:T(2,128)}, f32[2,2,768]{2,1,0:T(2,128)}, f32[2,2,768]{2,1,0:T(2,128)}) all-reduce(f32[2,2,768]{2,1,0:T(2,128)S(1)} %pad_maximum_fusion.4, f32[2,2,768]{2,1,0:T(2,128)S(1)} %pad_maximum_fusion.5, f32[2,2,768]{2,1,0:T(2,128)S(1)} %pad_maximum_fusion.7), channel_id=1, replica_groups=mesh['dp'=16,'tensor'=2] {'dp','tensor'}, use_global_device_ids=true, to_apply=%region_42.43 | all-reduce | flops 9216 | bytes 73728 | tf_op jit(solution)/shard_map/psum | solution.py:263
  1059.3 82.4 %all-reduce.7.cloned.1.call-done = (f32[2,384,768]{1,0,2:T(2,128)}, f32[2,1536,768]{1,0,2:T(2,128)}) async-done(((f32[2,384,768]{1,0,2:T(2,128)}, f32[2,1536,768]{1,0,2:T(2,128)}), (f32[2,384,768]{1,0,2:T(2,128)}, f32[2,1536,768]{1,0,2:T(2,128)})) %all-reduce.7.cloned.1.call-update) | async-done | bytes 11796496
  1145.3 112.4 %reduce-scatter.29.cloned.1.call-done = f32[2,48,1536]{2,1,0:T(8,128)} async-done(((f32[2,768,1536]{2,1,0:T(8,128)}), f32[2,48,1536]{2,1,0:T(8,128)}) %reduce-scatter.29.cloned.1.call-update) | async-done | bytes 589840 | tf_op jit(solution)/shard_map/reduce_scatter | solution.py:260
  1257.7 95.0 %reduce-scatter.27.cloned.1.call-done = f32[2,48,3,384]{3,1,2,0:T(8,128)} async-done(((f32[2,768,3,384]{3,1,2,0:T(8,128)}), f32[2,48,3,384]{3,1,2,0:T(8,128)}) %reduce-scatter.27.cloned.1.call-update) | async-done | bytes 442384 | tf_op jit(solution)/shard_map/reduce_scatter | solution.py:258
  (471 shorter events, 449.7 us)
Async XLA Ops:
  16.0 73.4 %all-gather.39.cloned.1.call-start = ((), (), s32[]{:S(2)}) async-start(), calls=%async_computation.28 | async-start | bytes 1880064 | tf_op jit(solution)/shard_map/all_gather | solution.py:127
  16.8 124.8 %reduce-scatter.11.cloned.1.call-start = ((), (), s32[]{:S(2)}) async-start(), calls=%async_computation.11 | async-start | bytes 2359296 | tf_op jit(solution)/shard_map/reduce_scatter | solution.py:143
  116.4 70.5 %all-gather.41.cloned.1.call-start = ((), (), s32[]{:S(2)}) async-start(), calls=%async_computation.29 | async-start | bytes 2506752 | tf_op jit(solution)/shard_map/all_gather | solution.py:129
  117.2 97.7 %all-gather.25.cloned.1.call-start = ((), (), s32[]{:S(2)}) async-start(), calls=%async_computation.12 | async-start | bytes 2359296 | tf_op jit(solution)/shard_map/all_gather | solution.py:153
  146.2 114.1 %all-gather.43.cloned.1.call-start = ((), (), s32[]{:S(2)}) async-start(), calls=%async_computation.30 | async-start | bytes 2506752 | tf_op jit(solution)/shard_map/all_gather | solution.py:130
  147.0 144.7 %reduce-scatter.13.cloned.1.call-start = ((), (), s32[]{:S(2)}) async-start(), calls=%async_computation.13 | async-start | bytes 2359296 | tf_op jit(solution)/shard_map/reduce_scatter | solution.py:158
  266.7 68.5 %all-gather.45.cloned.1.call-start = ((), (), s32[]{:S(2)}) async-start(), calls=%async_computation.31 | async-start | bytes 1880064 | tf_op jit(solution)/shard_map/all_gather | solution.py:127
  267.4 96.0 %all-gather.27.cloned.1.call-start = ((), (), s32[]{:S(2)}) async-start(), calls=%async_computation.14 | async-start | bytes 2359296 | tf_op jit(solution)/shard_map/all_gather | solution.py:136
  295.7 120.8 %reduce-scatter.15.cloned.1.call-start = ((), (), s32[]{:S(2)}) async-start(), calls=%async_computation.15 | async-start | bytes 2359296 | tf_op jit(solution)/shard_map/reduce_scatter | solution.py:143
  390.2 71.7 %all-gather.47.cloned.1.call-start = ((), (), s32[]{:S(2)}) async-start(), calls=%async_computation.32 | async-start | bytes 2506752 | tf_op jit(solution)/shard_map/all_gather | solution.py:129
  391.0 99.1 %all-gather.29.cloned.1.call-start = ((), (), s32[]{:S(2)}) async-start(), calls=%async_computation.16 | async-start | bytes 2359296 | tf_op jit(solution)/shard_map/all_gather | solution.py:153
  420.8 98.2 %all-gather.31.cloned.1.call-start = ((), (), s32[]{:S(2)}) async-start(), calls=%async_computation.18 | async-start | bytes 2359296 | tf_op jit(solution)/shard_map/all_gather | solution.py:211
  422.1 142.2 %all-gather.49.cloned.1.call-start = ((), (), s32[]{:S(2)}) async-start(), calls=%async_computation.33 | async-start | bytes 2506752 | tf_op jit(solution)/shard_map/all_gather | solution.py:130
  422.7 183.0 %reduce-scatter.19.cloned.1.call-start = ((), (), s32[]{:S(2)}) async-start(), calls=%async_computation.19 | async-start | bytes 2359296 | tf_op jit(solution)/shard_map/reduce_scatter | solution.py:220
  580.6 53.2 %reduce-scatter.17.cloned.1.call-start = ((), (), s32[]{:S(2)}) async-start(), calls=%async_computation.17 | async-start | bytes 2359296 | tf_op jit(solution)/shard_map/reduce_scatter | solution.py:158
  587.2 80.0 %all-gather.33.cloned.1.call-start = ((), (), s32[]{:S(2)}) async-start(), calls=%async_computation.20 | async-start | bytes 2359296 | tf_op jit(solution)/shard_map/all_gather | solution.py:232
  639.8 95.3 %reduce-scatter.21.cloned.1.call-start = ((), (), s32[]{:S(2)}) async-start(), calls=%async_computation.21 | async-start | bytes 2359296 | tf_op jit(solution)/shard_map/reduce_scatter | solution.py:241
  708.9 60.7 %all-gather.35.cloned.1.call-start = ((), (), s32[]{:S(2)}) async-start(), calls=%async_computation.22 | async-start | bytes 2359296 | tf_op jit(solution)/shard_map/all_gather | solution.py:211
  742.2 67.5 %reduce-scatter.23.cloned.1.call-start = ((), (), s32[]{:S(2)}) async-start(), calls=%async_computation.23 | async-start | bytes 2359296 | tf_op jit(solution)/shard_map/reduce_scatter | solution.py:220
  783.6 59.6 %all-gather.37.cloned.1.call-start = ((), (), s32[]{:S(2)}) async-start(), calls=%async_computation.24 | async-start | bytes 2359296 | tf_op jit(solution)/shard_map/all_gather | solution.py:232
  815.8 199.0 %reduce-scatter.25.cloned.1.call-start = ((), (), s32[]{:S(2)}) async-start(), calls=%async_computation.25 | async-start | bytes 2359296 | tf_op jit(solution)/shard_map/reduce_scatter | solution.py:241
  884.3 257.4 %all-reduce.7.cloned.1.call-start = ((), (), s32[]{:S(2)}) async-start(), calls=%async_computation.34 | async-start | bytes 23592960
  919.2 338.5 %reduce-scatter.29.cloned.1.call-start = ((), (), s32[]{:S(2)}) async-start(), calls=%async_computation.27 | async-start | bytes 10027008 | tf_op jit(solution)/shard_map/reduce_scatter | solution.py:260
  931.9 420.7 %reduce-scatter.27.cloned.1.call-start = ((), (), s32[]{:S(2)}) async-start(), calls=%async_computation.26 | async-start | bytes 7520256 | tf_op jit(solution)/shard_map/reduce_scatter | solution.py:258
  (100 other events, 2590.3 us)
Sparse Core Ops, SparseCore 0:
  16.1 29.9 all-gather.22
  48.9 40.3 all-gather.38
  116.5 24.9 reduce-scatter.10
  144.5 42.2 all-gather.40
  188.9 25.9 all-gather.24
  217.9 42.3 all-gather.42
  294.0 41.1 all-gather.44
  337.3 26.1 all-gather.26
  390.4 26.0 reduce-scatter.14
  419.6 42.3 all-gather.46
  464.0 25.9 all-gather.28
  491.6 27.2 all-gather.30
  521.9 42.3 all-gather.48
  580.8 24.8 reduce-scatter.18
  607.8 26.0 reduce-scatter.16
  639.9 27.1 all-gather.32
  709.0 26.0 reduce-scatter.20
  742.4 27.2 all-gather.34
  783.7 26.0 reduce-scatter.22
  815.9 27.2 all-gather.36
  884.4 26.0 reduce-scatter.24
  919.3 222.3 all-reduce.6
  1146.2 111.4 reduce-scatter.28
  1262.8 89.8 reduce-scatter.26
  (1 shorter events, 24.8 us)
where the time goes:
time: 1370 us; the launch traced here: 1360 us
  waiting for transfers between devices  844 us (62%)
  matrix products  176 us (13%)
  blocking collectives  155 us (11%)
  local copies, waits for them, and re-layouts  86.9 us (6%)
  other arithmetic  78.8 us (6%)
  between operations  16.6 us (1%)
    reduce_scatter x1, waiting for transfers between devices, body(): lax.psum_scatter(jnp.stack(grad_wup), 'dp', scatter_dimension=1, tiled=True)  112 us
    reduce_scatter x1, waiting for transfers between devices, body(): lax.psum_scatter(jnp.stack(grad_qkv), 'dp', scatter_dimension=1, tiled=True)  95 us
    unnamed x26, waiting for transfers between devices  84.7 us
    all_gather x2, waiting for transfers between devices, body(): lax.all_gather(up_weight[layer_index], 'dp', axis=0, tiled=True)  78.8 us
    all_gather x2, waiting for transfers between devices, body(): lax.all_gather(down_weight[layer_index], 'dp', axis=1, tiled=True)  70.7 us
    psum x1, blocking collectives, body(): lax.psum((jnp.stack(grad_qvb), jnp.stack(grad_upb)), 'dp')  64.8 us
    all_gather x2, waiting for transfers between devices, body(): lax.all_gather(qkv_weight[layer_index], 'dp', axis=0, tiled=True)  57.8 us
    all_gather x2, waiting for transfers between devices, body(): normed_mid = lax.all_gather(normed_mid_own, 'tensor', axis=0, tiled=True)  56.1 us
  transfers between devices with their start and end apart: 25, of which 24 were waited for; matrix products, arithmetic and copies ran while one was open for 10% of the time, Pallas kernels for 0%

commit v1 on v0

v1 whole, which is shorter than its diff:
```python
import functools

import jax
import jax.numpy as jnp
from jax import lax
from jax.experimental import pallas as pl
from jax.experimental.pallas import tpu as pltpu
from jax.sharding import PartitionSpec as P

HEAD_DIM = 64
EPSILON = 1e-06
MESH = pl.DeviceIdType.MESH
VMEM_LIMIT = 60 * 2**20
BF16 = jnp.bfloat16
F32 = jnp.float32
ITEM_COUNT = 8
GATHER_ORDER = (0, 1, 2, 3, 4, 5, 6, 7)
REDUCE_ORDER = (7, 6, 5, 4, 3, 2, 1, 0)


def places():
    dp = lax.axis_index("dp")
    y = lax.axis_index("tensor")
    return dp // 4, (dp // 2) % 2, dp % 2, y


def partners(z, x, k, y):
    def at(z_, x_, k_, y_):
        return {"dp": (z_ * 2 + x_) * 2 + k_, "tensor": y_}

    along_z = [at((z + step) % 4, x, k, y) for step in (1, 2, 3)]
    return along_z + [at(z, 1 - x, k, y), at(z, x, k, 1 - y), at(z, x, 1 - k, y)]


def greet(peers):
    barrier = pltpu.get_barrier_semaphore()
    for peer in peers:
        pl.semaphore_signal(barrier, inc=1, device_id=peer, device_id_type=MESH)
    pl.semaphore_wait(barrier, len(peers))


def gather_kernel(*refs):
    own, out = refs[:ITEM_COUNT], refs[ITEM_COUNT : 2 * ITEM_COUNT]
    held = refs[2 * ITEM_COUNT : 3 * ITEM_COUNT]
    send, recv, local = refs[3 * ITEM_COUNT :]
    z, x, k, y = places()
    peers = partners(z, x, k, y)
    mine = [
        pltpu.make_async_copy(own[i], held[i].at[y, z, x, k], local.at[i])
        for i in range(ITEM_COUNT)
    ]
    for copy in mine:
        copy.start()
    greet(peers)

    def remote(i, ref, slot, peer):
        return pltpu.make_async_remote_copy(
            ref, ref, send.at[i, slot], recv.at[i, slot], device_id=peers[peer], device_id_type=MESH
        )

    def copies(i, phase):
        b = held[i]
        if phase == 0:
            return [remote(i, b.at[y, z, x, k], j, j) for j in range(3)]
        if phase == 1:
            return [remote(i, b.at[y, 0:2, x, k], 3, 3), remote(i, b.at[y, 2:4, x, k], 4, 4)]
        if phase == 2:
            return [remote(i, b.at[y, 0:2, :, k], 5, 4), remote(i, b.at[:, 2:4, x, k], 6, 3)]
        return [remote(i, b.at[:, :, :, k], 7, 5)]

    live = {}

    def begin(i, phase):
        if phase == 0:
            mine[i].wait()
        live[i, phase] = copies(i, phase)
        for copy in live[i, phase]:
            copy.start()

    def finish(i, phase):
        for copy in live.pop((i, phase)):
            copy.wait()

    order = GATHER_ORDER
    begin(order[0], 0)
    begin(order[1], 0)
    back = []
    for turn in range(ITEM_COUNT + 3):
        for phase in (3, 2, 1, 0):
            spot = turn - phase
            if 0 <= spot < ITEM_COUNT:
                finish(order[spot], phase)
                if phase < 3:
                    begin(order[spot], phase + 1)
                else:
                    i = order[spot]
                    copy = pltpu.make_async_copy(held[i], out[i], local.at[i])
                    copy.start()
                    back.append(copy)
                if phase == 0 and spot + 2 < ITEM_COUNT:
                    begin(order[spot + 2], 0)
    for copy in back:
        copy.wait()


def gather_weights(shards):
    widths = [s.shape[-1] for s in shards]
    full = [(2, 4, 2, 2, 48, w) for w in widths]
    return pl.pallas_call(
        gather_kernel,
        out_shape=[jax.ShapeDtypeStruct(f, BF16) for f in full],
        in_specs=[pl.BlockSpec(memory_space=pl.ANY)] * ITEM_COUNT,
        out_specs=[pl.BlockSpec(memory_space=pl.ANY)] * ITEM_COUNT,
        scratch_shapes=[pltpu.VMEM(f, BF16) for f in full]
        + [
            pltpu.SemaphoreType.DMA((ITEM_COUNT, 8)),
            pltpu.SemaphoreType.DMA((ITEM_COUNT, 8)),
            pltpu.SemaphoreType.DMA((ITEM_COUNT,)),
        ],
        compiler_params=pltpu.CompilerParams(
            collective_id=0, has_side_effects=True, vmem_limit_bytes=VMEM_LIMIT
        ),
        name="gather_weights",
    )(*shards)


def add_into(target, source, blocks, width):
    for at_target, at_source in blocks:
        for start in range(0, width, 384):
            stop = pl.ds(start, 384)
            total = target[(*at_target, slice(None), stop)].astype(F32) + source[
                (*at_source, slice(None), stop)
            ].astype(F32)
            target[(*at_target, slice(None), stop)] = total.astype(target.dtype)


def reduce_kernel(*refs):
    n = ITEM_COUNT
    grads, out = refs[:n], refs[n : 2 * n]
    held, from_core, from_a, from_b, from_c, from_d, from_z = (
        refs[(2 + j) * n : (3 + j) * n] for j in range(7)
    )
    send, recv, local = refs[9 * n :]
    z, x, k, y = places()
    peers = partners(z, x, k, y)
    mine = [
        pltpu.make_async_copy(grads[i].at[:, :, :, k], held[i], local.at[i]) for i in range(n)
    ]
    for copy in mine:
        copy.start()
    greet(peers)

    def remote(i, source, target, slot, peer):
        return pltpu.make_async_remote_copy(
            source, target, send.at[i, slot], recv.at[i, slot], device_id=peers[peer], device_id_type=MESH
        )

    def copies(i, phase):
        b = held[i]
        if phase == 0:
            return [remote(i, grads[i].at[:, :, :, 1 - k], from_core[i], 0, 5)]
        if phase == 1:
            return [
                remote(i, b.at[1 - y, 0:2], from_a[i], 1, 4),
                remote(i, b.at[:, 2:4, 1 - x], from_b[i], 2, 3),
            ]
        if phase == 2:
            return [
                remote(i, b.at[y, 0:2, 1 - x], from_c[i], 3, 3),
                remote(i, b.at[1 - y, 2:4, x], from_d[i], 4, 4),
            ]
        return [
            remote(i, b.at[y, (z + 1 + j) % 4, x], from_z[i].at[j], 5 + j, j) for j in range(3)
        ]

    def total(i, phase):
        b = held[i]
        width = b.shape[-1]
        if phase == 0:
            mine[i].wait()

            def block(t, carry):
                at = (t // 8, (t // 2) % 4, t % 2)
                add_into(b, from_core[i], [(at, at)], width)
                return carry

            lax.fori_loop(0, 16, block, 0)
        elif phase == 1:
            def block(t, carry):
                p, q = t // 2, t % 2
                add_into(b, from_a[i], [((y, p, q), (p, q))], width)
                add_into(b, from_b[i], [((p, 2 + q, x), (p, q))], width)
                return carry

            lax.fori_loop(0, 4, block, 0)
        elif phase == 2:
            def block(t, carry):
                add_into(b, from_c[i], [((y, t, x), (t,))], width)
                add_into(b, from_d[i], [((y, 2 + t, x), (t,))], width)
                return carry

            lax.fori_loop(0, 2, block, 0)
        else:
            for start in range(0, width, 384):
                cols = pl.ds(start, 384)
                value = b[y, z, x, :, cols].astype(F32)
                for j in range(3):
                    value += from_z[i][j, :, cols].astype(F32)
                out[i][:, cols] = value

    live = {}

    def begin(i, phase):
        live[i, phase] = copies(i, phase)
        for copy in live[i, phase]:
            copy.start()

    def finish(i, phase):
        for copy in live.pop((i, phase)):
            copy.wait()
        total(i, phase)

    order = REDUCE_ORDER
    begin(order[0], 0)
    begin(order[1], 0)
    for turn in range(n + 3):
        for phase in (3, 2, 1, 0):
            spot = turn - phase
            if 0 <= spot < n:
                finish(order[spot], phase)
                if phase < 3:
                    begin(order[spot], phase + 1)
                if phase == 0 and spot + 2 < n:
                    begin(order[spot + 2], 0)


def reduce_gradients(grads):
    widths = [g.shape[-1] for g in grads]

    def scratch(*lead):
        return [pltpu.VMEM((*lead, 48, w), BF16) for w in widths]

    return pl.pallas_call(
        reduce_kernel,
        out_shape=[jax.ShapeDtypeStruct((48, w), F32) for w in widths],
        in_specs=[pl.BlockSpec(memory_space=pl.ANY)] * ITEM_COUNT,
        out_specs=[pl.BlockSpec(memory_space=pltpu.VMEM)] * ITEM_COUNT,
        scratch_shapes=scratch(2, 4, 2)
        + scratch(2, 4, 2)
        + scratch(2, 2)
        + scratch(2, 2)
        + scratch(2)
        + scratch(2)
        + scratch(3)
        + [
            pltpu.SemaphoreType.DMA((ITEM_COUNT, 8)),
            pltpu.SemaphoreType.DMA((ITEM_COUNT, 8)),
            pltpu.SemaphoreType.DMA((ITEM_COUNT,)),
        ],
        compiler_params=pltpu.CompilerParams(
            collective_id=1, has_side_effects=True, vmem_limit_bytes=VMEM_LIMIT
        ),
        name="reduce_gradients",
    )(*grads)


def layer_norm(inputs, gain_row, shift_row):
    centered = inputs - jnp.mean(inputs, axis=-1, keepdims=True)
    variance = jnp.mean(centered * centered, axis=-1, keepdims=True)
    return centered * lax.rsqrt(variance + EPSILON) * gain_row + shift_row


def gelu_exact(values):
    return jax.nn.gelu(values, approximate=False)


def mm(left, right, contract):
    return lax.dot_general(left, right, (contract, ((), ())), preferred_element_type=F32)


def halves(array):
    return jnp.stack(jnp.split(array, 2, axis=1))


def heads(array):
    return array.reshape(array.shape[0], -1, HEAD_DIM).transpose(1, 0, 2)


def flat(array):
    return array.transpose(1, 0, 2).reshape(array.shape[1], -1)


def body(use_kernels, dp_size, tokens, lengths, cotangent, norm_gain, norm_shift, qkv_weight, qv_bias,
         out_weight, up_weight, up_bias, down_weight, out_bias):
    part = lax.axis_index("tensor")
    layers = norm_gain.shape[0]
    rows, width = tokens.shape
    length = lax.dynamic_index_in_dim(lengths, part, keepdims=False)
    keep = jnp.arange(rows, dtype=jnp.int32) < length
    own = qkv_weight.shape[1]
    shards = []
    for layer in range(layers):
        shards += [
            qkv_weight[layer].reshape(own, -1),
            out_weight[layer].T,
            up_weight[layer],
            down_weight[layer].T,
        ]
    if use_kernels:
        full = [w.reshape(2, width, -1) for w in gather_weights(shards)]
    else:
        full = [
            lax.all_gather(s, ("tensor", "dp"), axis=0).reshape(2, width, -1) for s in shards
        ]
    qv_all = lax.all_gather(qv_bias, "tensor", axis=0)
    upb_all = lax.all_gather(up_bias, "tensor", axis=0)
    scale = HEAD_DIM**-0.5
    stream = tokens.astype(F32)
    saved = []
    for layer in range(layers):
        w_qkv, w_out, w_up, w_down = full[4 * layer : 4 * layer + 4]
        normed = layer_norm(stream, norm_gain[layer, 0], norm_shift[layer, 0]).astype(BF16)
        project = []
        for t in range(2):
            b = jnp.concatenate([qv_all[t, layer, 0], jnp.zeros_like(qv_all[t, layer, 0]), qv_all[t, layer, 1]])
            project.append((mm(normed, w_qkv[t], ((1,), (0,))) + b).astype(BF16))
        third = width // 2
        q, key, val = (
            heads(jnp.concatenate([project[t][:, j * third : (j + 1) * third] for t in range(2)], axis=1))
            for j in range(3)
        )
        scores = jnp.einsum("hqd,hkd->hqk", q, key, preferred_element_type=F32) * scale
        scores = jnp.where(keep[None, None, :], scores, -1e30)
        highest = jnp.max(scores, axis=-1, keepdims=True)
        exponent = jnp.exp(scores - highest)
        probs32 = exponent / jnp.sum(exponent, axis=-1, keepdims=True)
        probs = probs32.astype(BF16)
        attended = flat(jnp.einsum("hqk,hkd->hqd", probs, val, preferred_element_type=F32)).astype(BF16)
        branch = sum(mm(attended[:, t * third : (t + 1) * third], w_out[t], ((1,), (1,))) for t in range(2))
        middle = stream + branch + out_bias[layer, 0]
        normed_mid = layer_norm(middle, norm_gain[layer, 1], norm_shift[layer, 1]).astype(BF16)
        hidden = [mm(normed_mid, w_up[t], ((1,), (0,))) + upb_all[t, layer] for t in range(2)]
        activated = [gelu_exact(h).astype(BF16) for h in hidden]
        branch_mlp = sum(mm(activated[t], w_down[t], ((1,), (1,))) for t in range(2))
        saved.append((stream, middle, normed, q, key, val, probs, attended, normed_mid, hidden, activated))
        stream = middle + branch_mlp + out_bias[layer, 1]
    final = stream.astype(BF16)
    gradient = cotangent.astype(F32) * keep.astype(F32)[:, None]
    grads = [None] * (4 * layers)
    gain, shift, outb, qvb, upb = ([None] * layers for _ in range(5))
    for layer in reversed(range(layers)):
        stream_in, middle, normed, q, key, val, probs, attended, normed_mid, hidden, activated = saved[layer]
        w_qkv, w_out, w_up, w_down = full[4 * layer : 4 * layer + 4]
        third = width // 2
        bias_late = jnp.sum(gradient, axis=0)
        dout = gradient.astype(BF16)
        grads[4 * layer + 3] = jnp.stack([mm(dout, activated[t], ((0,), (0,))).astype(BF16) for t in range(2)])
        dhidden = []
        for t in range(2):
            dact = mm(dout, w_down[t], ((1,), (0,)))
            dhidden.append(jax.vjp(gelu_exact, hidden[t])[1](dact)[0].astype(BF16))
        upb[layer] = jnp.stack([jnp.sum(d.astype(F32), axis=0) for d in dhidden])
        grads[4 * layer + 2] = jnp.stack([mm(normed_mid, d, ((0,), (0,))).astype(BF16) for d in dhidden])
        dnormed_mid = sum(mm(dhidden[t], w_up[t], ((1,), (1,))) for t in range(2))
        pull = jax.vjp(layer_norm, middle, norm_gain[layer, 1], norm_shift[layer, 1])[1]
        dmid, gain_late, shift_late = pull(dnormed_mid)
        dmiddle = gradient + dmid
        bias_early = jnp.sum(dmiddle, axis=0)
        dbranch = dmiddle.astype(BF16)
        dout_t = mm(dbranch, attended, ((0,), (0,))).astype(BF16)
        grads[4 * layer + 1] = halves(dout_t)
        dattended = heads(jnp.concatenate([mm(dbranch, w_out[t], ((1,), (0,))) for t in range(2)], axis=1).astype(BF16))
        p = probs.astype(F32)
        dval = jnp.einsum("hqk,hqd->hkd", probs, dattended, preferred_element_type=F32)
        dprobs = jnp.einsum("hqd,hkd->hqk", dattended, val, preferred_element_type=F32)
        dscores = (p * (dprobs - jnp.sum(p * dprobs, axis=-1, keepdims=True))).astype(BF16)
        dquery = jnp.einsum("hqk,hkd->hqd", dscores, key, preferred_element_type=F32) * scale
        dkey = jnp.einsum("hqk,hqd->hkd", dscores, q, preferred_element_type=F32) * scale
        parts = [flat(a).astype(BF16) for a in (dquery, dkey, dval)]
        dproject = [
            jnp.concatenate([a[:, t * third : (t + 1) * third] for a in parts], axis=1) for t in range(2)
        ]
        qvb[layer] = jnp.stack([jnp.sum(parts[0].astype(F32), axis=0), jnp.sum(parts[2].astype(F32), axis=0)])
        grads[4 * layer] = jnp.stack([mm(normed, d, ((0,), (0,))).astype(BF16) for d in dproject])
        dnormed = sum(mm(dproject[t], w_qkv[t], ((1,), (1,))) for t in range(2))
        pull = jax.vjp(layer_norm, stream_in, norm_gain[layer, 0], norm_shift[layer, 0])[1]
        dfirst, gain_early, shift_early = pull(dnormed)
        gradient = dmiddle + dfirst
        gain[layer] = jnp.stack([gain_early, gain_late])
        shift[layer] = jnp.stack([shift_early, shift_late])
        outb[layer] = jnp.stack([bias_early, bias_late])
    if use_kernels:
        reduced = reduce_gradients([g.reshape(2, 4, 2, 2, 48, -1) for g in grads])
    else:
        reduced = [
            lax.psum_scatter(
                g.reshape(2 * dp_size, own, -1).astype(F32), ("tensor", "dp"), scatter_dimension=0
            )
            for g in grads
        ]
    g_gain, g_shift, g_outb, g_qvb, g_upb = lax.psum(
        (jnp.stack(gain), jnp.stack(shift), jnp.stack(outb), jnp.stack(qvb), jnp.stack(upb)),
        ("dp", "tensor"),
    )
    g_qvb = lax.dynamic_slice_in_dim(g_qvb, part * qv_bias.shape[2], qv_bias.shape[2], axis=2)
    g_upb = lax.dynamic_index_in_dim(g_upb, part, axis=1, keepdims=False)
    g_qkv = jnp.stack([reduced[4 * l].reshape(own, 3, -1) for l in range(layers)])
    g_out = jnp.stack([reduced[4 * l + 1].T for l in range(layers)])
    g_up = jnp.stack([reduced[4 * l + 2] for l in range(layers)])
    g_down = jnp.stack([reduced[4 * l + 3].T for l in range(layers)])
    return (final, gradient, g_gain, g_shift, g_qkv, g_qvb, g_out, g_up, g_upb, g_down, g_outb)


def solution(mesh):
    use_kernels = mesh.shape["dp"] == 16 and mesh.shape["tensor"] == 2
    return jax.shard_map(
        functools.partial(body, use_kernels, mesh.shape["dp"]),
        mesh=mesh,
        in_specs=(
            P(("dp", "tensor"), None),
            P("dp"),
            P(("dp", "tensor"), None),
            P(),
            P(),
            P(None, "dp", None, "tensor"),
            P(None, None, "tensor"),
            P(None, "tensor", "dp"),
            P(None, "dp", "tensor"),
            P(None, "tensor"),
            P(None, "tensor", "dp"),
            P(),
        ),
        out_specs=(
            P(("dp", "tensor"), None),
            P(("dp", "tensor"), None),
            P(),
            P(),
            P(None, "dp", None, "tensor"),
            P(None, None, "tensor"),
            P(None, "tensor", "dp"),
            P(None, "dp", "tensor"),
            P(None, "tensor"),
            P(None, "tensor", "dp"),
            P(),
        ),
        check_vma=False,
    )
```

time: 1370 us -> 625 us (0.46)
  waiting for transfers between devices: 844 us -> 0.02 us
  Pallas kernels: 0 us -> 288 us
  blocking collectives: 155 us -> 10.1 us
  matrix products: 176 us -> 157 us
  other arithmetic: 78.8 us -> 63.8 us
    all_gather x14 -> x0, waiting for transfers between devices: 385 us -> none  [the longest x2 78.8 us: body(): lax.all_gather(up_weight[layer_index], 'dp', axis=0, tiled=True)]
    reduce_scatter x10 -> x0, waiting for transfers between devices: 375 us -> none  [the longest x1 112 us: body(): lax.psum_scatter(jnp.stack(grad_wup), 'dp', scatter_dimension=1, tiled=True)]
    pallas_call x0 -> x2, Pallas kernels: none -> 288 us  [the longest x1 146 us: reduce_gradients(): pl.pallas_call(reduce_kernel, out_shape=[jax.ShapeDtypeStruct((48, w), F3...]
    psum x2 -> x0, blocking collectives: 104 us -> none  [the longest x1 64.8 us: body(): lax.psum((jnp.stack(grad_qvb), jnp.stack(grad_upb)), 'dp')]
    unnamed x26 -> x1, waiting for transfers between devices: 84.7 us -> 0.02 us
    all_gather x2, blocking collectives: 51.1 us -> 10.1 us  [the longest x1 5.55 us: body(): qv_all = lax.all_gather(qv_bias, 'tensor', axis=0)]
    dot_general x52 -> x56, matrix products: 176 us -> 142 us  [the longest x46 107 us: mm(): lax.dot_general(left, right, (contract, ((), ())), preferred_element_type...]
    while x12 -> x0, local copies, waits for them, and re-layouts: 17.7 us -> none  [the longest x4 11.7 us: attend_back(): grads = lax.map(one_clip, (blocks, upstream_blocks, log_total, key_mask))]
  transfers between devices with their start and end apart: 25 -> 1, of which waited for: 24 -> 0; matrix products, arithmetic and copies ran while one was open for 10% -> 9% of each run, Pallas kernels for 0% -> 24%
where the time goes in v1:
time: 625 us; the launch traced here: 618 us
  Pallas kernels  288 us (46%)
  matrix products  157 us (25%)
  local copies, waits for them, and re-layouts  82.3 us (13%)
  other arithmetic  63.8 us (10%)
  between operations  17 us (3%)
  blocking collectives  10.1 us (2%)
    pallas_call x1, Pallas kernels, reduce_gradients(): pl.pallas_call(reduce_kernel, out_shape=[jax.ShapeDtypeStruct((48, w), F3...  146 us
    pallas_call x1, Pallas kernels, gather_weights(): pl.pallas_call(gather_kernel, out_shape=[jax.ShapeDtypeStruct(f, BF16) fo...  141 us
    dot_general x46, matrix products, mm(): lax.dot_general(left, right, (contract, ((), ())), preferred_element_type...  107 us
    unnamed x374, local copies, waits for them, and re-layouts  25.9 us
    sub x2, matrix products, body(): exponent = jnp.exp(scores - highest)  15.2 us
    convert_element_type x2, other arithmetic, body(): (p * (dprobs - jnp.sum(p * dprobs, axis=-1, keepdims=True))).astype(BF16)  14.1 us
    dot_general x2, matrix products, body(): jnp.einsum('hqd,hkd->hqk', dattended, val, preferred_element_type=F32)  13.4 us
    convert_element_type x2, other arithmetic, body(): probs = probs32.astype(BF16)  12.9 us
  transfers between devices with their start and end apart: 1, of which 0 were waited for; matrix products, arithmetic and copies ran while one was open for 9% of the time, Pallas kernels for 24%

profile of v1, /device:TPU:0, one launch (start us, length us, event | category | flops | bytes accessed | tf_op | source)
XLA Modules:
  0.0 617.8 jit_solution(8299680081109238071)
XLA Ops:
  12.6 5.5 all-gather
  19.6 4.6 all-gather.2
  30.2 141.1 %gather_weights.1 = (bf16[2,4,2,2,48,1152]{5,4,3,2,1,0:T(8,128)(2,1)}, bf16[2,4,2,2,48,384]{5,4,3,2,1,0:T(8,128)(2,1)}, bf16[2,4,2,2,48,1536]{5,4,3,2,1,0:T(8,12...) custom-call(bf16[48,1152]{1,0:T(8,128)(2,1)} %bitcast.352, ...), custom_call_target="tpu_custom_call" | custom-call | tf_op jit(solution)/shard_map/gather_weights/pallas_call | solution.py:109
  171.4 5.5 fusion.135
  182.0 3.1 fusion.139
  187.5 7.7 %fusion.152 = (f32[12,512]{1,0:T(8,128)S(1)}, f32[12,512,512]{1,2,0:T(8,128)}) fusion(pred[512]{0:T(512)(128)(4,1)S(1)} %get-tuple-element.234, bf16[12,512,64]{1,2,0:T(8,128)(2,1)S(1)} %bitcast.341, bf16[12,512,64]{1,2,0:T(8,128)(2,1)S(1)} %bitcast.279), kind=kOutput, calls=%fused_computation.353 | convolution fusion | flops 415236608 | bytes 14180864 | tf_op jit(solution)/shard_map/sub | solution.py:335
  195.2 6.4 %divide_convert_fusion.1 = bf16[12,512,512]{1,2,0:T(8,128)(2,1)S(1)} fusion(f32[12,512,512]{1,2,0:T(8,128)} %get-tuple-element.189, f32[12,512]{1,0:T(8,128)S(1)} %get-tuple-element.188), kind=kLoop, calls=%fused_computation.13 | loop fusion | flops 6291456 | bytes 18898944 | tf_op jit(solution)/shard_map/convert_element_type | solution.py:337
  207.4 4.3 fusion.133
  212.1 9.8 %multiply_convert_fusion.2 = (bf16[512,1536]{1,0:T(8,128)(2,1)S(1)}, f32[512,1536]{1,0:T(8,128)}, f32[512,1536]{1,0:T(8,128)}) fusion(f32[1536]{0:T(1024)S(1)} %get-tuple-element.80, bf16[512,768]{1,0:T(8,128)(2,1)S(1)} %add_convert_fusion.7, bf16[768,1536]{1,0:T(8,128)(2,1)S(1)} %bitcast.305), kind=kOutput, calls=%fused_computation.92 | convolution fusion | flops 1259864064 | bytes 11016192 | tf_op jit(solution)/shard_map/dot_general | solution.py:278
  222.0 10.3 %multiply_convert_fusion.3 = (bf16[512,1536]{1,0:T(8,128)(2,1)S(1)}, f32[512,1536]{1,0:T(8,128)}, f32[512,1536]{1,0:T(8,128)}) fusion(f32[1536]{0:T(1024)S(1)} %get-tuple-element.81, bf16[512,768]{1,0:T(8,128)(2,1)S(1)} %add_convert_fusion.7, bf16[768,1536]{1,0:T(8,128)(2,1)S(1)} %bitcast.309), kind=kOutput, calls=%fused_computation.105 | convolution fusion | flops 1259864064 | bytes 11016192 | tf_op jit(solution)/shard_map/dot_general | solution.py:278
  243.6 7.5 %fusion.155 = (f32[12,512]{1,0:T(8,128)S(1)}, f32[12,512,512]{1,2,0:T(8,128)}) fusion(pred[512]{0:T(512)(128)(4,1)S(1)} %get-tuple-element.234, bf16[12,512,64]{1,2,0:T(8,128)(2,1)S(1)} %bitcast.343, bf16[12,512,64]{1,2,0:T(8,128)(2,1)S(1)} %bitcast.281), kind=kOutput, calls=%fused_computation.356 | convolution fusion | flops 415236608 | bytes 14180864 | tf_op jit(solution)/shard_map/sub | solution.py:335
  251.1 6.4 %divide_convert_fusion = bf16[12,512,512]{1,2,0:T(8,128)(2,1)S(1)} fusion(f32[12,512,512]{1,2,0:T(8,128)} %get-tuple-element.197, f32[12,512]{1,0:T(8,128)S(1)} %get-tuple-element.196), kind=kLoop, calls=%fused_computation.10 | loop fusion | flops 6291456 | bytes 18898944 | tf_op jit(solution)/shard_map/convert_element_type | solution.py:337
  265.2 9.4 %multiply_convert_fusion.1 = (bf16[512,1536]{1,0:T(8,128)(2,1)}, f32[512,1536]{1,0:T(8,128)S(1)}, f32[512,1536]{1,0:T(8,128)S(1)}) fusion(f32[1536]{0:T(1024)S(1)} %get-tuple-element.79, bf16[512,768]{1,0:T(8,128)(2,1)S(1)} %add_convert_fusion.5, bf16[768,1536]{1,0:T(8,128)(2,1)S(1)} %bitcast.315), kind=kOutput, calls=%fused_computation.79 | convolution fusion | flops 1259864064 | bytes 11016192 | tf_op jit(solution)/shard_map/dot_general | solution.py:278
  274.6 2.9 convert_reduce_fusion.1
  279.0 9.5 %multiply_convert_fusion = (bf16[512,1536]{1,0:T(8,128)(2,1)}, f32[512,1536]{1,0:T(8,128)S(1)}, f32[512,1536]{1,0:T(8,128)S(1)}) fusion(f32[1536]{0:T(1024)S(1)} %copy-done.147, bf16[512,768]{1,0:T(8,128)(2,1)S(1)} %add_convert_fusion.5, bf16[768,1536]{1,0:T(8,128)(2,1)S(1)} %bitcast.313), kind=kOutput, calls=%fused_computation.66 | convolution fusion | flops 1259864064 | bytes 11016192 | tf_op jit(solution)/shard_map/dot_general | solution.py:278
  297.4 3.5 convert_reduce_fusion.5
  301.0 6.7 %fusion.2 = (f32[12,512]{1,0:T(8,128)S(1)}, f32[12,512,512]{1,2,0:T(8,128)}) fusion(bf16[12,512,512]{1,2,0:T(8,128)(2,1)S(1)} %divide_convert_fusion, bf16[12,512,64]{1,2,0:T(8,128)(2,1)S(1)} %bitcast.272, bf16[512,6,64]{0,2,1:T(8,128)(2,1)S(1)} %convolution_convert_fusion.20, bf16[512,6,64]{0,2,1:T(8,128)(2,1)S(1)} %convolution_convert_fusion.21), kind=kOutput, calls=%fused_computation.6 | convolution fusion | flops 412477440 | bytes 20471808 | tf_op jit(solution)/shard_map/hqd,hkd->hqk/dot_general | solution.py:375
  307.7 7.3 %fusion.3 = bf16[12,512,512]{1,2,0:T(8,128)(2,1)S(1)} fusion(f32[12,512,512]{1,2,0:T(8,128)} %get-tuple-element.204, f32[12,512]{1,0:T(8,128)S(1)} %get-tuple-element.203, f32[12,512,512]{1,2,0:T(8,128)S(1)} %bitcast.268, f32[12,512]{1,0:T(8,128)S(1)} %get-tuple-element.196), kind=kLoop, calls=%fused_computation.7 | loop fusion | flops 18874368 | bytes 31506432 | tf_op jit(solution)/shard_map/convert_element_type | solution.py:376
  346.8 3.5 convert_reduce_fusion.7
  350.3 6.7 %fusion.4 = (f32[12,512]{1,0:T(8,128)S(1)}, f32[12,512,512]{1,2,0:T(8,128)}) fusion(bf16[12,512,512]{1,2,0:T(8,128)(2,1)S(1)} %bitcast.264, bf16[12,512,64]{1,2,0:T(8,128)(2,1)S(1)} %bitcast.270, bf16[512,6,64]{0,2,1:T(8,128)(2,1)S(1)} %convolution_convert_fusion.18, bf16[512,6,64]{0,2,1:T(8,128)(2,1)S(1)} %convolution_convert_fusion.19), kind=kOutput, calls=%fused_computation.8 | convolution fusion | flops 412477440 | bytes 20471808 | tf_op jit(solution)/shard_map/hqd,hkd->hqk/dot_general | solution.py:375
  357.0 6.8 %fusion.5 = bf16[12,512,512]{1,2,0:T(8,128)(2,1)S(1)} fusion(f32[12,512,512]{1,2,0:T(8,128)} %get-tuple-element.208, f32[12,512]{1,0:T(8,128)S(1)} %get-tuple-element.207, f32[12,512,512]{1,2,0:T(8,128)S(1)} %bitcast.266, f32[12,512]{1,0:T(8,128)S(1)} %copy-done.102), kind=kLoop, calls=%fused_computation.9 | loop fusion | flops 18874368 | bytes 31506432 | tf_op jit(solution)/shard_map/convert_element_type | solution.py:376
  399.6 3.2 convolution_convert_fusion.2
  447.1 146.4 %reduce_gradients.1 = (f32[48,1152]{1,0:T(8,128)}, f32[48,384]{1,0:T(8,128)}, f32[48,1536]{1,0:T(8,128)}, f32[48,1536]{1,0:T(8,128)}, f32[48,1152]{1,0:T(8,128)}...) custom-call(bf16[2,4,2,2,48,1152]{5,4,3,2,1,0:T(8,128)(2,1)} %pad_maximum_fusion.4.refs_0_, ...), custom_call_target="tpu_custom_call" | custom-call | tf_op jit(solution)/shard_map/reduce_gradients/pallas_call | solution.py:243
  595.6 5.0 add_convert_fusion.4
  (556 shorter events, 177.5 us)
Async XLA Ops:
  7.2 21.5 %copy-start.95 = (bf16[2,48,1536]{2,1,0:T(8,128)(2,1)S(1)}, bf16[2,48,1536]{2,1,0:T(8,128)(2,1)}, u32[]{:S(2)}) copy-start(bf16[2,48,1536]{2,1,0:T(8,128)(2,1)} %param.20) | copy-start | bytes 884740
  7.2 22.2 %copy-start.96 = (bf16[2,1536,48]{1,2,0:T(8,128)(2,1)S(1)}, bf16[2,1536,48]{1,2,0:T(8,128)(2,1)}, u32[]{:S(2)}) copy-start(bf16[2,1536,48]{1,2,0:T(8,128)(2,1)} %param.22) | copy-start | bytes 884740
  7.2 22.9 %copy-start.128 = (f32[2,2,768]{2,1,0:T(2,128)S(1)}, f32[2,2,768]{2,1,0:T(2,128)}, u32[]{:S(2)}) copy-start(f32[2,2,768]{2,1,0:T(2,128)} %param.16) | copy-start | bytes 36868
  7.2 22.9 %copy-start.129 = (f32[2,2,768]{2,1,0:T(2,128)S(1)}, f32[2,2,768]{2,1,0:T(2,128)}, u32[]{:S(2)}) copy-start(f32[2,2,768]{2,1,0:T(2,128)} %param.15) | copy-start | bytes 36868
  7.2 596.7 %all-reduce.3.cloned.1.call-start = ((), (), s32[]{:S(2)}) async-start(), calls=%async_computation | async-start | bytes 147456 | tf_op jit(solution)/shard_map/psum | solution.py:401
  8.6 169.8 %copy-start.110 = (f32[512]{0:T(512)}, f32[512]{0:T(512)S(1)}, u32[]{:S(2)}) copy-start(f32[512]{0:T(512)S(1)} %broadcast_multiply_fusion.3) | copy-start | bytes 6148
  10.1 166.7 %copy-start.122 = (f32[512]{0:T(512)}, f32[512]{0:T(512)S(1)}, u32[]{:S(2)}) copy-start(f32[512]{0:T(512)S(1)} %fusion.51) | copy-start | bytes 6148
  10.2 168.2 %copy-start.117 = (f32[512]{0:T(512)}, f32[512]{0:T(512)S(1)}, u32[]{:S(2)}) copy-start(f32[512]{0:T(512)S(1)} %fusion.78) | copy-start | bytes 6148
  30.2 148.2 %copy-start.106 = (f32[768]{0:T(1024)}, f32[768]{0:T(1024)S(1)}, u32[]{:S(2)}) copy-start(f32[768]{0:T(1024)S(1)} %get-tuple-element.231) | copy-start | bytes 9220
  30.2 148.2 %copy-start.150 = (f32[768]{0:T(1024)}, f32[768]{0:T(1024)S(1)}, u32[]{:S(2)}) copy-start(f32[768]{0:T(1024)S(1)} %get-tuple-element.92) | copy-start | bytes 9220
  30.2 181.6 %copy-start.108 = (f32[768]{0:T(1024)}, f32[768]{0:T(1024)S(1)}, u32[]{:S(2)}) copy-start(f32[768]{0:T(1024)S(1)} %get-tuple-element.232) | copy-start | bytes 9220
  207.0 26.7 %copy-start.5 = (f32[512,768]{1,0:T(8,128)}, f32[512,768]{1,0:T(8,128)S(1)}, u32[]{:S(2)}) copy-start(f32[512,768]{1,0:T(8,128)S(1)} %get-tuple-element.191) | copy-start | bytes 4718596
  211.7 10.2 %copy-start.41 = (bf16[1,4,2,2,48,1536]{5,4,3,2,1,0:T(8,128)(2,1)}, bf16[1,4,2,2,48,1536]{5,4,3,2,1,0:T(8,128)(2,1)S(1)}, u32[]{:S(2)}) copy-start(bf16[1,4,2,2,48,1536]{5,4,3,2,1,0:T(8,128)(2,1)S(1)} %get-tuple-element.225) | copy-start | bytes 7077892
  211.7 10.2 %copy-start.45 = (bf16[1,4,2,2,48,1536]{5,4,3,2,1,0:T(8,128)(2,1)}, bf16[1,4,2,2,48,1536]{5,4,3,2,1,0:T(8,128)(2,1)S(1)}, u32[]{:S(2)}) copy-start(bf16[1,4,2,2,48,1536]{5,4,3,2,1,0:T(8,128)(2,1)S(1)} %get-tuple-element.224) | copy-start | bytes 7077892
  211.7 20.5 %copy-start.47 = (bf16[1,4,2,2,48,1536]{5,4,3,2,1,0:T(8,128)(2,1)}, bf16[1,4,2,2,48,1536]{5,4,3,2,1,0:T(8,128)(2,1)S(1)}, u32[]{:S(2)}) copy-start(bf16[1,4,2,2,48,1536]{5,4,3,2,1,0:T(8,128)(2,1)S(1)} %get-tuple-element.136) | copy-start | bytes 7077892
  211.8 22.0 %copy-start.43 = (bf16[1,4,2,2,48,1536]{5,4,3,2,1,0:T(8,128)(2,1)}, bf16[1,4,2,2,48,1536]{5,4,3,2,1,0:T(8,128)(2,1)S(1)}, u32[]{:S(2)}) copy-start(bf16[1,4,2,2,48,1536]{5,4,3,2,1,0:T(8,128)(2,1)S(1)} %get-tuple-element.135) | copy-start | bytes 7077892
  222.0 11.8 %copy-start.166 = (bf16[512,1536]{1,0:T(8,128)(2,1)}, bf16[512,1536]{1,0:T(8,128)(2,1)S(1)}, u32[]{:S(2)}) copy-start(bf16[512,1536]{1,0:T(8,128)(2,1)S(1)} %get-tuple-element.127) | copy-start | bytes 4718596
  263.2 30.5 %copy-start.3 = (f32[512,768]{1,0:T(8,128)}, f32[512,768]{1,0:T(8,128)S(1)}, u32[]{:S(2)}) copy-start(f32[512,768]{1,0:T(8,128)S(1)} %get-tuple-element.199) | copy-start | bytes 4718596
  264.8 23.6 %copy-start.38 = (bf16[1,4,2,2,48,1536]{5,4,3,2,1,0:T(8,128)(2,1)}, bf16[1,4,2,2,48,1536]{5,4,3,2,1,0:T(8,128)(2,1)S(1)}, u32[]{:S(2)}) copy-start(bf16[1,4,2,2,48,1536]{5,4,3,2,1,0:T(8,128)(2,1)S(1)} %get-tuple-element.131) | copy-start | bytes 7077892
  265.1 13.8 %copy-start.69 = (bf16[512,768]{1,0:T(8,128)(2,1)}, bf16[512,768]{1,0:T(8,128)(2,1)S(1)}, u32[]{:S(2)}) copy-start(bf16[512,768]{1,0:T(8,128)(2,1)S(1)} %add_convert_fusion.5) | copy-start | bytes 2359300
  297.4 10.3 %slice-start.5 = ((s8[12582912]{0:T(1024)(128)(4,1)}), s8[4194304]{0:T(1024)(128)(4,1)S(1)}, s32[]{:S(2)}) async-start(s8[12582912]{0:T(1024)(128)(4,1)} %bitcast.267), calls=%async_computation.6 | async-start | bytes 8388608
  346.7 10.2 %slice-start.2 = ((s8[12582912]{0:T(1024)(128)(4,1)}), s8[4194304]{0:T(1024)(128)(4,1)S(1)}, s32[]{:S(2)}) async-start(s8[12582912]{0:T(1024)(128)(4,1)} %bitcast.265), calls=%async_computation.3 | async-start | bytes 8388608
  447.1 148.5 %copy-start.4 = (f32[512,768]{1,0:T(8,128)S(1)}, f32[512,768]{1,0:T(8,128)}, u32[]{:S(2)}) copy-start(f32[512,768]{1,0:T(8,128)} %copy-done.3) | copy-start | bytes 4718596
  447.1 148.5 %copy-start.152 = (f32[768]{0:T(1024)S(1)}, f32[768]{0:T(1024)}, u32[]{:S(2)}) copy-start(f32[768]{0:T(1024)} %get-tuple-element.82) | copy-start | bytes 9220
  (161 other events, 483.9 us)
Sparse Core Ops, SparseCore 0:
  399.7 128.9 all-reduce.2

commit v2 on v1

--- a/solution.py
+++ b/solution.py
@@ -290,7 +290,328 @@
     return array.transpose(1, 0, 2).reshape(array.shape[1], -1)
 
 
-def body(use_kernels, dp_size, tokens, lengths, cotangent, norm_gain, norm_shift, qkv_weight, qv_bias,
+def run_pump(events):
+    queue = list(events)
+
+    def step(count):
+        for _ in range(min(count, len(queue))):
+            queue.pop(0)[1]()
+
+    def need(tag):
+        if any(name == tag for name, _ in queue):
+            while True:
+                name, act = queue.pop(0)
+                act()
+                if name == tag:
+                    break
+
+    return need, step
+
+
+def gather_events(own, held, send, recv, local, peers, place):
+    z, x, k, y = place
+    n = len(held)
+    mine = [
+        pltpu.make_async_copy(own[i], held[i].at[y, z, x, k], local.at[i]) for i in range(n)
+    ]
+    for copy in mine:
+        copy.start()
+
+    def remote(i, ref, slot, peer):
+        return pltpu.make_async_remote_copy(
+            ref, ref, send.at[i, slot], recv.at[i, slot], device_id=peers[peer], device_id_type=MESH
+        )
+
+    def copies(i, phase):
+        b = held[i]
+        if phase == 0:
+            return [remote(i, b.at[y, z, x, k], j, j) for j in range(3)]
+        if phase == 1:
+            return [remote(i, b.at[y, 0:2, x, k], 3, 3), remote(i, b.at[y, 2:4, x, k], 4, 4)]
+        if phase == 2:
+            return [remote(i, b.at[y, 0:2, :, k], 5, 4), remote(i, b.at[:, 2:4, x, k], 6, 3)]
+        return [remote(i, b.at[:, :, :, k], 7, 5)]
+
+    live = {}
+
+    def begin(i, phase):
+        if phase == 0:
+            mine[i].wait()
+        live[i, phase] = copies(i, phase)
+        for copy in live[i, phase]:
+            copy.start()
+
+    def finish(i, phase):
+        for copy in live.pop((i, phase)):
+            copy.wait()
+
+    order = GATHER_ORDER
+    events = []
+
+    def event(spot, phase):
+        i = order[spot]
+
+        def act():
+            finish(i, phase)
+            if phase < 3:
+                begin(i, phase + 1)
+            if phase == 0 and spot + 2 < n:
+                begin(order[spot + 2], 0)
+
+        return (("w", i) if phase == 3 else None, act)
+
+    for turn in range(n + 3):
+        for phase in (3, 2, 1, 0):
+            if 0 <= turn - phase < n:
+                events.append(event(turn - phase, phase))
+
+    def start():
+        begin(order[0], 0)
+        begin(order[1], 0)
+
+    return start, events
+
+
+def matrix(ref, *lead):
+    value = ref[lead] if lead else ref[...]
+    return value.reshape(-1, value.shape[-1])
+
+
+def norm_rows(source, gain_row, shift_row, target):
+    def block(t, carry):
+        rows = pl.ds(pl.multiple_of(t * 128, 128), 128)
+        target[rows, :] = layer_norm(source[rows, :], gain_row, shift_row).astype(BF16)
+        return carry
+
+    lax.fori_loop(0, source.shape[0] // 128, block, 0)
+
+
+def turn_rows(source, target, k):
+    for c in range(2):
+        turned = source[:, c * 384 : (c + 1) * 384].T
+        for j in range(8):
+            block = c * 8 + j
+            target[(block + k) % 2, block // 4, (block // 2) % 2] = turned[j * 48 : (j + 1) * 48]
+
+
+def forward_kernel(*refs):
+    n = ITEM_COUNT
+    it = iter(refs)
+
+    def take(count):
+        return [next(it) for _ in range(count)]
+
+    own = take(n)
+    tokens, lengths, gain, shift, outb, qvb, upb = take(7)
+    whole = take(n)
+    saved = [take(9) for _ in range(2)]
+    (final,) = take(1)
+    held = take(n)
+    (stream, middle, normed, turned, turned_mid, project, attended, active, slope, probs, qv_all, up_all) = take(12)
+    send, recv, local, out_sem, prob_sem, small_send, small_recv, whole_sem = take(8)
+    place = z, x, k, y = places()
+    peers = partners(z, x, k, y)
+    start, events = gather_events(own, held, send, recv, local, peers, place)
+    need, step = run_pump(events)
+    qv_all[y] = qvb[...]
+    up_all[y] = upb[...]
+    greet(peers)
+    start()
+    small = [
+        pltpu.make_async_remote_copy(
+            ref.at[y], ref.at[y], small_send.at[j], small_recv.at[j], device_id=peers[4], device_id_type=MESH
+        )
+        for j, ref in enumerate((qv_all, up_all))
+    ]
+    for copy in small:
+        copy.start()
+    stream[...] = tokens[...].astype(F32)
+    length = lengths[y]
+    rows = stream.shape[0]
+    outgoing = {}
+
+    def save(layer, slot, ref):
+        copy = pltpu.make_async_copy(ref, saved[layer][slot], out_sem.at[layer, slot])
+        copy.start()
+        outgoing[slot] = copy
+
+    def settle(slot):
+        if slot in outgoing:
+            outgoing.pop(slot).wait()
+
+    back = []
+
+    def keep_weight(i):
+        copy = pltpu.make_async_copy(held[i], whole[i], whole_sem.at[i])
+        copy.start()
+        back.append(copy)
+
+    for layer in range(2):
+        w_qkv, w_out, w_up, w_down = held[4 * layer : 4 * layer + 4]
+        settle(2)
+        norm_rows(stream, gain[layer, 0:1], shift[layer, 0:1], normed)
+        turn_rows(normed, turned, k)
+        save(layer, 0, stream)
+        save(layer, 2, turned)
+        if layer == 0:
+            for copy in small:
+                copy.wait()
+        need(("w", 4 * layer))
+        keep_weight(4 * layer)
+        settle(4)
+        for half in range(2):
+            for t in range(3):
+                part = mm(normed[...], matrix(w_qkv, half, slice(None), slice(None), slice(None), slice(None), pl.ds(t * 384, 384)), ((1,), (0,)))
+                if t != 1:
+                    part = part + qv_all[half, layer, t // 2 : t // 2 + 1]
+                project[half, :, t * 384 : (t + 1) * 384] = part.astype(BF16)
+        save(layer, 4, project)
+        step(1)
+        settle(5)
+
+        def pair(j, carry):
+            half = j // 3
+            at = (j % 3) * 128
+            lane = lax.broadcasted_iota(jnp.int32, (1, 128), 1) < 64
+            query = project[half, :, pl.ds(pl.multiple_of(at, 128), 128)]
+            key = project[half, :, pl.ds(pl.multiple_of(at + 384, 128), 128)]
+            value = project[half, :, pl.ds(pl.multiple_of(at + 768, 128), 128)]
+            value_t = value.T
+            hidden_key = lax.broadcasted_iota(jnp.int32, (rows, 1), 0) >= length
+            both = []
+            slot = j % 2
+            for h in range(2):
+                here = lane if h == 0 else jnp.logical_not(lane)
+                some = jnp.where(here, key, jnp.zeros_like(key)) * jnp.asarray(HEAD_DIM**-0.5, BF16)
+                scores = mm(some, query, ((1,), (1,)))
+                scores = jnp.where(hidden_key, -1e30, scores)
+                exponent = jnp.exp(scores - jnp.max(scores, axis=0, keepdims=True))
+                prob = (exponent * (1.0 / jnp.sum(exponent, axis=0, keepdims=True))).astype(BF16)
+                probs[j, h] = prob
+                both.append(mm(value_t[h * 64 : (h + 1) * 64], prob, ((1,), (0,))))
+            block = jnp.concatenate(both, axis=0).T
+            attended[:, pl.ds(pl.multiple_of(j * 128, 128), 128)] = block.astype(BF16)
+            return carry
+
+        settle(6)
+        for j0 in range(0, 6, 3):
+            lax.fori_loop(j0, j0 + 3, pair, 0)
+            step(1)
+        save(layer, 5, attended)
+        save(layer, 6, probs)
+        need(("w", 4 * layer + 1))
+        keep_weight(4 * layer + 1)
+        settle(1)
+        for c in range(2):
+            cols = slice(c * 384, (c + 1) * 384)
+            total = stream[:, cols] + outb[layer, 0:1, cols]
+            for half in range(2):
+                total += mm(attended[:, half * 384 : (half + 1) * 384], matrix(w_out, half, slice(2 * c, 2 * c + 2)), ((1,), (1,)))
+            middle[:, cols] = total
+        save(layer, 1, middle)
+        settle(3)
+        norm_rows(middle, gain[layer, 1:2], shift[layer, 1:2], normed)
+        turn_rows(normed, turned_mid, k)
+        save(layer, 3, turned_mid)
+        step(1)
+        need(("w", 4 * layer + 2))
+        keep_weight(4 * layer + 2)
+        settle(7)
+        settle(8)
+
+        def unit(t, carry):
+            half = t // 3
+            cols = pl.ds(pl.multiple_of((t % 3) * 512, 128), 512)
+            hidden = mm(normed[...], matrix(w_up, half, slice(None), slice(None), slice(None), slice(None), cols), ((1,), (0,)))
+            hidden = hidden + up_all[half, layer : layer + 1, cols]
+            cdf = 0.5 * (1.0 + lax.erf(hidden * (0.5**0.5)))
+            density = jnp.exp(-0.5 * hidden * hidden) * 0.3989422804014327
+            active[half, :, cols] = (hidden * cdf).astype(BF16)
+            slope[half, :, cols] = (cdf + hidden * density).astype(BF16)
+            return carry
+
+        for t0 in range(0, 6, 3):
+            lax.fori_loop(t0, t0 + 3, unit, 0)
+            step(1)
+        save(layer, 7, active)
+        save(layer, 8, slope)
+        need(("w", 4 * layer + 3))
+        keep_weight(4 * layer + 3)
+        settle(0)
+        for c in range(2):
+            cols = slice(c * 384, (c + 1) * 384)
+            total = middle[:, cols] + outb[layer, 1:2, cols]
+            for half in range(2):
+                total += mm(active[half], matrix(w_down, half, slice(2 * c, 2 * c + 2)), ((1,), (1,)))
+            stream[:, cols] = total
+        step(1)
+    final[...] = stream[...].astype(BF16)
+    for slot in list(outgoing):
+        settle(slot)
+    for copy in back:
+        copy.wait()
+
+
+def forward(shards, tokens, lengths, gain, shift, outb, qvb, upb):
+    rows, width = tokens.shape
+    widths = [s.shape[-1] for s in shards]
+    full = [(2, 4, 2, 2, 48, w) for w in widths]
+    layer_saves = [
+        ((rows, width), F32),
+        ((rows, width), F32),
+        ((2, 4, 2, 48, rows), BF16),
+        ((2, 4, 2, 48, rows), BF16),
+        ((2, rows, widths[0]), BF16),
+        ((rows, width), BF16),
+        ((6, 2, rows, rows), BF16),
+        ((2, rows, widths[2]), BF16),
+        ((2, rows, widths[2]), BF16),
+    ]
+    any_spec = pl.BlockSpec(memory_space=pl.ANY)
+    vmem_spec = pl.BlockSpec(memory_space=pltpu.VMEM)
+    out_shape = (
+        [jax.ShapeDtypeStruct(f, BF16) for f in full]
+        + [jax.ShapeDtypeStruct(s, t) for s, t in layer_saves * 2]
+        + [jax.ShapeDtypeStruct((rows, width), BF16)]
+    )
+    by_slot = {j: pltpu.VMEM(*layer_saves[j]) for j in range(9)}
+    outs = pl.pallas_call(
+        forward_kernel,
+        out_shape=out_shape,
+        in_specs=[any_spec] * ITEM_COUNT + [vmem_spec, pl.BlockSpec(memory_space=pltpu.SMEM)] + [vmem_spec] * 5,
+        out_specs=[any_spec] * (ITEM_COUNT + 18) + [vmem_spec],
+        scratch_shapes=[pltpu.VMEM(f, BF16) for f in full]
+        + [
+            by_slot[0],
+            by_slot[1],
+            pltpu.VMEM((rows, width), BF16),
+            by_slot[2],
+            by_slot[3],
+            by_slot[4],
+            by_slot[5],
+            by_slot[7],
+            by_slot[8],
+            by_slot[6],
+            pltpu.VMEM((2, *qvb.shape), F32),
+            pltpu.VMEM((2, *upb.shape), F32),
+            pltpu.SemaphoreType.DMA((ITEM_COUNT, 8)),
+            pltpu.SemaphoreType.DMA((ITEM_COUNT, 8)),
+            pltpu.SemaphoreType.DMA((ITEM_COUNT,)),
+            pltpu.SemaphoreType.DMA((2, 9)),
+            pltpu.SemaphoreType.DMA((2,)),
+            pltpu.SemaphoreType.DMA((2,)),
+            pltpu.SemaphoreType.DMA((2,)),
+            pltpu.SemaphoreType.DMA((ITEM_COUNT,)),
+        ],
+        compiler_params=pltpu.CompilerParams(
+            collective_id=0, has_side_effects=True, vmem_limit_bytes=VMEM_LIMIT
+        ),
+        name="forward",
+    )(*shards, tokens, lengths, gain, shift, outb, qvb, upb)
+    return outs[:ITEM_COUNT], [outs[ITEM_COUNT + 9 * l : ITEM_COUNT + 9 * l + 9] for l in range(2)], outs[-1]
+
+
+def generic_body(dp_size, tokens, lengths, cotangent, norm_gain, norm_shift, qkv_weight, qv_bias,
          out_weight, up_weight, up_bias, down_weight, out_bias):
     part = lax.axis_index("tensor")
     layers = norm_gain.shape[0]
@@ -306,7 +627,7 @@
             up_weight[layer],
             down_weight[layer].T,
         ]
-    if use_kernels:
+    if False:
         full = [w.reshape(2, width, -1) for w in gather_weights(shards)]
     else:
         full = [
@@ -389,7 +710,7 @@
         gain[layer] = jnp.stack([gain_early, gain_late])
         shift[layer] = jnp.stack([shift_early, shift_late])
         outb[layer] = jnp.stack([bias_early, bias_late])
-    if use_kernels:
+    if False:
         reduced = reduce_gradients([g.reshape(2, 4, 2, 2, 48, -1) for g in grads])
     else:
         reduced = [
@@ -411,10 +732,102 @@
     return (final, gradient, g_gain, g_shift, g_qkv, g_qvb, g_out, g_up, g_upb, g_down, g_outb)
 
 
+def fused_body(tokens, lengths, cotangent, norm_gain, norm_shift, qkv_weight, qv_bias, out_weight, up_weight,
+               up_bias, down_weight, out_bias):
+    part = lax.axis_index("tensor")
+    layers = norm_gain.shape[0]
+    rows, width = tokens.shape
+    third = width // 2
+    own = qkv_weight.shape[1]
+    length = lax.dynamic_index_in_dim(lengths, part, keepdims=False)
+    keep = jnp.arange(rows, dtype=jnp.int32) < length
+    shards = []
+    for layer in range(layers):
+        shards += [
+            qkv_weight[layer].reshape(own, -1),
+            out_weight[layer].T,
+            up_weight[layer],
+            down_weight[layer].T,
+        ]
+    full, saved, final = forward(shards, tokens, lengths, norm_gain, norm_shift, out_bias, qv_bias, up_bias)
+    full = [w.reshape(2, width, -1) for w in full]
+    gradient = cotangent.astype(F32) * keep.astype(F32)[:, None]
+    grads = [None] * (4 * layers)
+    gain, shift, outb, qvb, upb = ([None] * layers for _ in range(5))
+    scale = HEAD_DIM**-0.5
+    for layer in reversed(range(layers)):
+        stream_in, middle, _, _, project, attended, probs_t, activated, slope = saved[layer]
+        w_qkv, w_out, w_up, w_down = full[4 * layer : 4 * layer + 4]
+        normed = layer_norm(stream_in, norm_gain[layer, 0], norm_shift[layer, 0]).astype(BF16)
+        normed_mid = layer_norm(middle, norm_gain[layer, 1], norm_shift[layer, 1]).astype(BF16)
+        q, key, val = (
+            heads(jnp.concatenate([project[t][:, j * third : (j + 1) * third] for t in range(2)], axis=1))
+            for j in range(3)
+        )
+        probs = probs_t.reshape(-1, rows, rows).transpose(0, 2, 1)
+        bias_late = jnp.sum(gradient, axis=0)
+        dout = gradient.astype(BF16)
+        grads[4 * layer + 3] = jnp.stack([mm(dout, activated[t], ((0,), (0,))).astype(BF16) for t in range(2)])
+        dhidden = []
+        for t in range(2):
+            dact = mm(dout, w_down[t], ((1,), (0,)))
+            dhidden.append((dact * slope[t].astype(F32)).astype(BF16))
+        upb[layer] = jnp.stack([jnp.sum(d.astype(F32), axis=0) for d in dhidden])
+        grads[4 * layer + 2] = jnp.stack([mm(normed_mid, d, ((0,), (0,))).astype(BF16) for d in dhidden])
+        dnormed_mid = sum(mm(dhidden[t], w_up[t], ((1,), (1,))) for t in range(2))
+        pull = jax.vjp(layer_norm, middle, norm_gain[layer, 1], norm_shift[layer, 1])[1]
+        dmid, gain_late, shift_late = pull(dnormed_mid)
+        dmiddle = gradient + dmid
+        bias_early = jnp.sum(dmiddle, axis=0)
+        dbranch = dmiddle.astype(BF16)
+        dout_t = mm(dbranch, attended, ((0,), (0,))).astype(BF16)
+        grads[4 * layer + 1] = halves(dout_t)
+        dattended = heads(jnp.concatenate([mm(dbranch, w_out[t], ((1,), (0,))) for t in range(2)], axis=1).astype(BF16))
+        p = probs.astype(F32)
+        dval = jnp.einsum("hqk,hqd->hkd", probs, dattended, preferred_element_type=F32)
+        dprobs = jnp.einsum("hqd,hkd->hqk", dattended, val, preferred_element_type=F32)
+        dscores = (p * (dprobs - jnp.sum(p * dprobs, axis=-1, keepdims=True))).astype(BF16)
+        dquery = jnp.einsum("hqk,hkd->hqd", dscores, key, preferred_element_type=F32) * scale
+        dkey = jnp.einsum("hqk,hqd->hkd", dscores, q, preferred_element_type=F32) * scale
+        parts = [flat(a).astype(BF16) for a in (dquery, dkey, dval)]
+        dproject = [
+            jnp.concatenate([a[:, t * third : (t + 1) * third] for a in parts], axis=1) for t in range(2)
+        ]
+        qvb[layer] = jnp.stack([jnp.sum(parts[0].astype(F32), axis=0), jnp.sum(parts[2].astype(F32), axis=0)])
+        grads[4 * layer] = jnp.stack([mm(normed, d, ((0,), (0,))).astype(BF16) for d in dproject])
+        dnormed = sum(mm(dproject[t], w_qkv[t], ((1,), (1,))) for t in range(2))
+        pull = jax.vjp(layer_norm, stream_in, norm_gain[layer, 0], norm_shift[layer, 0])[1]
+        dfirst, gain_early, shift_early = pull(dnormed)
+        gradient = dmiddle + dfirst
+        gain[layer] = jnp.stack([gain_early, gain_late])
+        shift[layer] = jnp.stack([shift_early, shift_late])
+        outb[layer] = jnp.stack([bias_early, bias_late])
+    if True:
+        reduced = reduce_gradients([g.reshape(2, 4, 2, 2, 48, -1) for g in grads])
+    else:
+        reduced = [
+            lax.psum_scatter(
+                g.reshape(2 * 32, own, -1).astype(F32), ("tensor", "dp"), scatter_dimension=0
+            )
+            for g in grads
+        ]
+    g_gain, g_shift, g_outb, g_qvb, g_upb = lax.psum(
+        (jnp.stack(gain), jnp.stack(shift), jnp.stack(outb), jnp.stack(qvb), jnp.stack(upb)),
+        ("dp", "tensor"),
+    )
+    g_qvb = lax.dynamic_slice_in_dim(g_qvb, part * qv_bias.shape[2], qv_bias.shape[2], axis=2)
+    g_upb = lax.dynamic_index_in_dim(g_upb, part, axis=1, keepdims=False)
+    g_qkv = jnp.stack([reduced[4 * l].reshape(own, 3, -1) for l in range(layers)])
+    g_out = jnp.stack([reduced[4 * l + 1].T for l in range(layers)])
+    g_up = jnp.stack([reduced[4 * l + 2] for l in range(layers)])
+    g_down = jnp.stack([reduced[4 * l + 3].T for l in range(layers)])
+    return (final, gradient, g_gain, g_shift, g_qkv, g_qvb, g_out, g_up, g_upb, g_down, g_outb)
+
+
 def solution(mesh):
     use_kernels = mesh.shape["dp"] == 16 and mesh.shape["tensor"] == 2
     return jax.shard_map(
-        functools.partial(body, use_kernels, mesh.shape["dp"]),
+        fused_body if use_kernels else functools.partial(generic_body, mesh.shape["dp"]),
         mesh=mesh,
         in_specs=(
             P(("dp", "tensor"), None),

time: 625 us -> 572 us (0.915)
  matrix products: 157 us -> 95.1 us
  blocking collectives: 10.1 us -> 0 us
  Pallas kernels: 288 us -> 298 us
    dot_general x46 -> x30, matrix products: 107 us -> 50.7 us  [mm(): lax.dot_general(left, right, (contract, ((), ())), preferred_element_type...]
    sub x2 -> x0, matrix products: 15.2 us -> none  [body(): exponent = jnp.exp(scores - highest)]
    convert_element_type x8 -> x4, other arithmetic: 28 us -> 16.2 us  [the longest x2 15.4 us: fused_body(): (p * (dprobs - jnp.sum(p * dprobs, axis=-1, keepdims=True))).astype(BF16)]
    pallas_call x1, Pallas kernels: 141 us -> 152 us  [forward(): pl.pallas_call(forward_kernel, out_shape=out_shape, in_specs=[any_spec] *...]
    concatenate x6, local copies, waits for them, and re-layouts: 3.45 us -> 13.7 us  [fused_body(): jnp.concatenate([project[t][:, j * third:(j + 1) * third] for t in range(...]
    all_gather x2 -> x0, blocking collectives: 10.1 us -> none  [the longest x1 5.55 us: body(): qv_all = lax.all_gather(qv_bias, 'tensor', axis=0)]
    dot_general x10 -> x8, matrix products: 35.1 us -> 44.4 us  [the longest x2 20.5 us: fused_body(): jnp.einsum('hqd,hkd->hqk', dattended, val, preferred_element_type=F32)]
    unnamed x374 -> x289, local copies, waits for them, and re-layouts: 25.9 us -> 17.2 us
  transfers between devices with their start and end apart: 1 -> 1, of which waited for: 0 -> 0; matrix products, arithmetic and copies ran while one was open for 9% -> 9% of each run, Pallas kernels for 24% -> 26%
where the time goes in v2:
time: 572 us; the launch traced here: 562 us
  Pallas kernels  298 us (52%)
  matrix products  95.1 us (17%)
  local copies, waits for them, and re-layouts  82.9 us (14%)
  other arithmetic  69.9 us (12%)
  between operations  16 us (3%)
    pallas_call x1, Pallas kernels, forward(): pl.pallas_call(forward_kernel, out_shape=out_shape, in_specs=[any_spec] *...  152 us
    pallas_call x1, Pallas kernels, reduce_gradients(): pl.pallas_call(reduce_kernel, out_shape=[jax.ShapeDtypeStruct((48, w), F3...  146 us
    dot_general x30, matrix products, mm(): lax.dot_general(left, right, (contract, ((), ())), preferred_element_type...  50.7 us
    dot_general x2, matrix products, fused_body(): jnp.einsum('hqd,hkd->hqk', dattended, val, preferred_element_type=F32)  20.5 us
    unnamed x289, local copies, waits for them, and re-layouts  17.2 us
    convert_element_type x2, other arithmetic, fused_body(): (p * (dprobs - jnp.sum(p * dprobs, axis=-1, keepdims=True))).astype(BF16)  15.4 us
    concatenate x6, local copies, waits for them, and re-layouts, fused_body(): jnp.concatenate([project[t][:, j * third:(j + 1) * third] for t in range(...  13.7 us
  transfers between devices with their start and end apart: 1, of which 0 were waited for; matrix products, arithmetic and copies ran while one was open for 9% of the time, Pallas kernels for 26%

profile of v2, /device:TPU:0, one launch (start us, length us, event | category | flops | bytes accessed | tf_op | source)
XLA Modules:
  0.0 561.6 jit_solution(16006114580056929039)
XLA Ops:
  14.3 151.8 %forward.1 = (bf16[2,4,2,2,48,1152]{5,4,3,2,1,0:T(8,128)(2,1)}, bf16[2,4,2,2,48,384]{5,4,3,2,1,0:T(8,128)(2,1)}, bf16[2,4,2,2,48,1536]{5,4,3,2,1,0:T(8,128)(2,1)...) custom-call(bf16[48,1152]{1,0:T(8,128)(2,1)} %bitcast.311, ...), custom_call_target="tpu_custom_call" | custom-call | tf_op jit(solution)/shard_map/forward/pallas_call | solution.py:578
  170.3 4.5 fusion.62
  180.8 2.4 multiply_reduce_fusion
  189.0 2.7 fusion.55
  193.3 5.6 %convert_reduce_fusion.4 = (f32[12,64]{1,0:T(8,128)}, bf16[12,512,64]{1,2,0:T(8,128)(2,1)S(1)}) fusion(bf16[12,512,512]{2,1,0:T(8,128)(2,1)} %bitcast.260, bf16[512,6,64]{0,2,1:T(8,128)(2,1)S(1)} %convolution_convert_fusion.18, bf16[512,6,64]{0,2,1:T(8,128)(2,1)S(1)} %convolution_convert_fusion.19), kind=kOutput, calls=%fused_computation.46 | convolution fusion | flops 404225280 | bytes 7867392 | tf_op jit(solution)/shard_map/hqk,hqd->hkd/dot_general | solution.py:787
  207.0 10.2 %fusion.2 = (f32[12,512]{1,0:T(8,128)}, f32[12,512,512]{1,2,0:T(8,128)}) fusion(bf16[6,2,512,512]{3,2,1,0:T(8,128)(2,1)} %get-tuple-element.47, bf16[12,512,64]{1,2,0:T(8,128)(2,1)} %bitcast.269, bf16[512,6,64]{0,2,1:T(8,128)(2,1)S(1)} %convolution_convert_fusion.18, bf16[512,6,64]{0,2,1:T(8,128)(2,1)} %copy-done.23), kind=kOutput, calls=%fused_computation.6 | convolution fusion | flops 412477440 | bytes 20471808 | tf_op jit(solution)/shard_map/hqd,hkd->hqk/dot_general | solution.py:788
  220.4 7.7 %fusion.3 = bf16[12,512,512]{1,2,0:T(8,128)(2,1)S(1)} fusion(f32[12,512,512]{1,2,0:T(8,128)} %get-tuple-element.182, f32[12,512]{1,0:T(8,128)S(1)} %copy-done.79, bf16[6,2,512,512]{3,2,1,0:T(8,128)(2,1)} %get-tuple-element.47), kind=kLoop, calls=%fused_computation.7 | loop fusion | flops 12582912 | bytes 25190400 | tf_op jit(solution)/shard_map/convert_element_type | solution.py:789
  235.3 4.3 convert_reduce_fusion.5
  240.4 2.4 fusion.64
  254.1 4.9 fusion.60
  271.8 2.8 fusion.53
  276.2 5.6 convert_reduce_fusion.6
  288.6 10.2 %fusion = (f32[12,512]{1,0:T(8,128)}, f32[12,512,512]{1,2,0:T(8,128)}) fusion(bf16[6,2,512,512]{3,2,1,0:T(8,128)(2,1)} %get-tuple-element.56, bf16[12,512,64]{1,2,0:T(8,128)(2,1)} %bitcast.270, bf16[512,6,64]{0,2,1:T(8,128)(2,1)S(1)} %convolution_convert_fusion.16, bf16[512,6,64]{0,2,1:T(8,128)(2,1)} %copy-done.24), kind=kOutput, calls=%fused_computation.2 | convolution fusion | flops 412477440 | bytes 20471808 | tf_op jit(solution)/shard_map/hqd,hkd->hqk/dot_general | solution.py:788
  302.1 7.7 %fusion.1 = bf16[12,512,512]{1,2,0:T(8,128)(2,1)S(1)} fusion(f32[12,512,512]{1,2,0:T(8,128)} %get-tuple-element.186, f32[12,512]{1,0:T(8,128)S(1)} %copy-done.80, bf16[6,2,512,512]{3,2,1,0:T(8,128)(2,1)} %get-tuple-element.56), kind=kLoop, calls=%fused_computation.3 | loop fusion | flops 12582912 | bytes 25190400 | tf_op jit(solution)/shard_map/convert_element_type | solution.py:789
  317.1 4.3 convert_reduce_fusion.7
  326.0 3.3 multiply_reduce_fusion.3
  347.5 3.3 convolution_convert_fusion.10
  360.0 2.7 convolution_convert_fusion.4
  362.8 2.8 convolution_convert_fusion.5
  380.9 2.6 pad_maximum_fusion.refs_2_
  383.5 2.8 pad_maximum_fusion.1.refs_3_
  390.4 2.6 pad_maximum_fusion.2.refs_6_
  393.0 2.5 pad_maximum_fusion.3.refs_7_
  395.6 145.9 %reduce_gradients.1 = (f32[48,1152]{1,0:T(8,128)}, f32[48,384]{1,0:T(8,128)}, f32[48,1536]{1,0:T(8,128)}, f32[48,1536]{1,0:T(8,128)}, f32[48,1152]{1,0:T(8,128)}...) custom-call(bf16[2,4,2,2,48,1152]{5,4,3,2,1,0:T(8,128)(2,1)} %pad_maximum_fusion.4.refs_0_, ...), custom_call_target="tpu_custom_call" | custom-call | tf_op jit(solution)/shard_map/reduce_gradients/pallas_call | solution.py:243
  (436 shorter events, 150.0 us)
Async XLA Ops:
  7.2 6.4 %copy-start.83 = (f32[2,2,768]{2,1,0:T(2,128)S(1)}, f32[2,2,768]{2,1,0:T(2,128)}, u32[]{:S(2)}) copy-start(f32[2,2,768]{2,1,0:T(2,128)} %refs_10_.1) | copy-start | bytes 36868
  7.2 6.4 %copy-start.84 = (f32[2,2,768]{2,1,0:T(2,128)S(1)}, f32[2,2,768]{2,1,0:T(2,128)}, u32[]{:S(2)}) copy-start(f32[2,2,768]{2,1,0:T(2,128)} %refs_11_.1) | copy-start | bytes 36868
  7.2 541.8 %all-reduce.3.cloned.1.call-start = ((), (), s32[]{:S(2)}) async-start(), calls=%async_computation | async-start | bytes 147456 | tf_op jit(solution)/shard_map/psum | solution.py:814
  14.3 169.0 %copy-start.98 = (f32[768]{0:T(1024)}, f32[768]{0:T(1024)S(1)}, u32[]{:S(2)}) copy-start(f32[768]{0:T(1024)S(1)} %get-tuple-element.219) | copy-start | bytes 9220
  167.8 78.6 %copy-start.87 = (f32[512]{0:T(512)}, f32[512]{0:T(512)S(1)}, u32[]{:S(2)}) copy-start(f32[512]{0:T(512)S(1)} %broadcast_multiply_fusion.2) | copy-start | bytes 6148
  168.4 14.8 %copy-start.85 = (f32[512]{0:T(512)}, f32[512]{0:T(512)S(1)}, u32[]{:S(2)}) copy-start(f32[512]{0:T(512)S(1)} %broadcast_multiply_fusion.3) | copy-start | bytes 6148
  168.9 14.3 %copy-start.109 = (f32[512]{0:T(512)}, f32[512]{0:T(512)S(1)}, u32[]{:S(2)}) copy-start(f32[512]{0:T(512)S(1)} %fusion.27) | copy-start | bytes 6148
  170.3 18.7 %copy-start.107 = (f32[512]{0:T(512)}, f32[512]{0:T(512)S(1)}, u32[]{:S(2)}) copy-start(f32[512]{0:T(512)S(1)} %fusion.26) | copy-start | bytes 6148
  193.3 5.7 %copy-start.23 = (bf16[512,6,64]{0,2,1:T(8,128)(2,1)}, bf16[512,6,64]{0,2,1:T(8,128)(2,1)S(1)}, u32[]{:S(2)}) copy-start(bf16[512,6,64]{0,2,1:T(8,128)(2,1)S(1)} %convolution_convert_fusion.19) | copy-start | bytes 1179652
  193.3 6.6 %copy-start.27 = (bf16[2,512,1152]{2,1,0:T(8,128)(2,1)S(1)}, bf16[2,512,1152]{2,1,0:T(8,128)(2,1)}, u32[]{:S(2)}) copy-start(bf16[2,512,1152]{2,1,0:T(8,128)(2,1)} %get-tuple-element.58) | copy-start | bytes 7077892
  193.3 6.6 %copy-start.28 = (bf16[2,512,1152]{2,1,0:T(8,128)(2,1)S(1)}, bf16[2,512,1152]{2,1,0:T(8,128)(2,1)}, u32[]{:S(2)}) copy-start(bf16[2,512,1152]{2,1,0:T(8,128)(2,1)} %get-tuple-element.49) | copy-start | bytes 7077892
  206.9 10.2 %copy-start.38 = (bf16[512,384]{1,0:T(8,128)(2,1)S(1)}, bf16[512,384]{1,0:T(8,128)(2,1)}, u32[]{:S(2)}) copy-start(bf16[512,384]{1,0:T(8,128)(2,1)} %get-tuple-element.155) | copy-start | bytes 1179652
  207.0 10.2 %copy-start.39 = (bf16[512,384]{1,0:T(8,128)(2,1)S(1)}, bf16[512,384]{1,0:T(8,128)(2,1)}, u32[]{:S(2)}) copy-start(bf16[512,384]{1,0:T(8,128)(2,1)} %get-tuple-element.152) | copy-start | bytes 1179652
  220.4 7.8 %copy-start.48 = (bf16[512,768]{0,1:T(8,128)(2,1)S(1)}, bf16[512,768]{0,1:T(8,128)(2,1)}, u32[]{:S(2)}) copy-start(bf16[512,768]{0,1:T(8,128)(2,1)} %copy.48) | copy-start | bytes 2359300
  231.7 11.1 %copy-start.58 = (bf16[512,384]{0,1:T(8,128)(2,1)}, bf16[512,384]{0,1:T(8,128)(2,1)S(1)}, u32[]{:S(2)}) copy-start(bf16[512,384]{0,1:T(8,128)(2,1)S(1)} %get-tuple-element.169) | copy-start | bytes 1179652
  249.9 17.5 %copy-start.92 = (f32[512]{0:T(512)}, f32[512]{0:T(512)S(1)}, u32[]{:S(2)}) copy-start(f32[512]{0:T(512)S(1)} %broadcast_multiply_fusion.1) | copy-start | bytes 6148
  251.9 17.2 %copy-start.94 = (f32[512]{0:T(512)}, f32[512]{0:T(512)S(1)}, u32[]{:S(2)}) copy-start(f32[512]{0:T(512)S(1)} %get-tuple-element.204) | copy-start | bytes 6148
  251.9 15.5 %copy-start.113 = (f32[512]{0:T(512)}, f32[512]{0:T(512)S(1)}, u32[]{:S(2)}) copy-start(f32[512]{0:T(512)S(1)} %fusion.29) | copy-start | bytes 6148
  254.1 7.0 %copy-start.52 = (bf16[512,768]{1,0:T(8,128)(2,1)}, bf16[512,768]{1,0:T(8,128)(2,1)S(1)}, u32[]{:S(2)}) copy-start(bf16[512,768]{1,0:T(8,128)(2,1)S(1)} %convert_element_type.250) | copy-start | bytes 2359300
  288.6 10.2 %copy-start.37 = (bf16[512,384]{1,0:T(8,128)(2,1)S(1)}, bf16[512,384]{1,0:T(8,128)(2,1)}, u32[]{:S(2)}) copy-start(bf16[512,384]{1,0:T(8,128)(2,1)} %get-tuple-element.147) | copy-start | bytes 1179652
  288.6 10.2 %copy-start.40 = (bf16[512,384]{1,0:T(8,128)(2,1)S(1)}, bf16[512,384]{1,0:T(8,128)(2,1)}, u32[]{:S(2)}) copy-start(bf16[512,384]{1,0:T(8,128)(2,1)} %get-tuple-element.144) | copy-start | bytes 1179652
  302.1 7.7 %copy-start.49 = (bf16[512,768]{0,1:T(8,128)(2,1)S(1)}, bf16[512,768]{0,1:T(8,128)(2,1)}, u32[]{:S(2)}) copy-start(bf16[512,768]{0,1:T(8,128)(2,1)} %copy.55) | copy-start | bytes 2359300
  317.1 6.8 %copy-start.32 = (bf16[1,4,2,2,48,1152]{5,4,3,2,1,0:T(8,128)(2,1)S(1)}, bf16[1,4,2,2,48,1152]{5,4,3,2,1,0:T(8,128)(2,1)}, u32[]{:S(2)}) copy-start(bf16[1,4,2,2,48,1152]{5,4,3,2,1,0:T(8,128)(2,1)} %get-tuple-element.132) | copy-start | bytes 5308420
  395.6 148.7 %copy-start.14 = (f32[512,768]{1,0:T(8,128)S(1)}, f32[512,768]{1,0:T(8,128)}, u32[]{:S(2)}) copy-start(f32[512,768]{1,0:T(8,128)} %get-tuple-element.116) | copy-start | bytes 4718596
  (118 other events, 281.2 us)
Sparse Core Ops, SparseCore 0:
  347.5 125.9 all-reduce.2
